TPU v7x, 512 devices: a whole 4x4x16 slice. The times are simulated.
512 devices in a mesh: page: 64 (over x, z), head: 8 (over y, core).
Axes of the slice: x: 4, y: 4, z: 16, core: 2. Of those that a mesh axis runs over, the one named last changes fastest.
Arguments:
- hidden: bfloat16 [24576, 4096], P('page'), may hold values from -6 to 6
- attention_norm_gain: bfloat16 [4096], replicated, may hold values from 0.25 to 1.75
- wq: bfloat16 [4096, 4096], P('page', 'head'), may hold values from -0.09375 to 0.09375
- adapter_down_weight: bfloat16 [4096, 1024], P('head', 'page'), may hold values from -0.09375 to 0.09375
- adapter_up_weight: bfloat16 [1024, 4096], P('page', 'head'), may hold values from -0.75 to 0.75
- key_value_cache: bfloat16 [24576, 2, 1024], P('page', None, 'head'), may hold values from -110 to 110
- logical_page_table: int32 [64, 3], P('page'), may hold values from 0 to 2, each once within a row
- lengths: int32 [16], replicated, may hold values from 1 to 6144, 24576 in all
- prompt_adapter_index: int32 [16], replicated, may hold values from 0 to 63
Outputs:
- queries: bfloat16 [24576, 4096], P('page', 'head')
- attended: bfloat16 [24576, 4096], P('page', 'head')
Inputs may be any that keep to these rules, and one draw needn't show every extreme that they name: The lengths sum to 24576 and the longest is exactly 6144. `logical_page_table`: each row is a permutation of the page slots of one index of page.
All inputs are finite; a program needn't handle non-finite values.
Results may differ from a plain program's by a relative error of at most 0.012.
The roundings to bfloat16 on the way count: a program that leaves them out, or rounds other values in their place, can miss the bound.
Values may be sent and summed in bfloat16 or wider, within the bound.
A program may use at most 128 MiB of HBM per device.

v0:
```python
import math

import jax
import jax.numpy as jnp
from jax import lax
from jax.sharding import PartitionSpec as P

HEAD_WIDTH = 128
ADAPTER_RANK = 16


EPSILON = 1e-05
ROPE_BASE = 500000.0


def from_behind(value, axis, steps):
    count = lax.axis_size(axis)
    leading, last = (max(0, -steps), min(count, count - steps))
    return lax.ppermute(value, axis, [(source, source + steps) for source in range(leading, last)])


def apply_rotation(values_f, token_position, head_size):
    half = head_size // 2
    inverse = ROPE_BASE ** (-(jnp.arange(half, dtype=jnp.float32) * 2.0 / head_size))
    angle = token_position.astype(jnp.float32)[:, None] * inverse[None, :]
    cosine = jnp.cos(angle)[:, None, :]
    sine = jnp.sin(angle)[:, None, :]
    first = values_f[..., :half]
    second = values_f[..., half:]
    return jnp.concatenate(
        [first * cosine - second * sine, second * cosine + first * sine], axis=-1
    )


def score_block(query, keyblock):
    return lax.dot_general(
        query, keyblock, (((1,), (1,)), ((), ())), preferred_element_type=jnp.float32
    )


def mix_block(weights, valueblock):
    return jnp.dot(weights, valueblock, preferred_element_type=jnp.float32)


def normalize(scores, visible, inv_scale):
    scores = jnp.where(visible, scores * inv_scale, -jnp.inf)
    top = jnp.max(scores, axis=-1, keepdims=True)
    expo = jnp.exp(scores - top)
    return (expo / jnp.sum(expo, axis=-1, keepdims=True)).astype(jnp.bfloat16)


def body(
    hidden,
    attention_norm_gain,
    wq,
    adapter_down_weight,
    adapter_up_weight,
    key_value_cache,
    logical_page_table,
    lengths,
    prompt_adapter_index,
):
    token_device_rows = hidden.shape[0]
    page_index = lax.axis_index("page")
    head_index = lax.axis_index("head")
    span_count = lax.axis_size("page") // 4
    x = hidden.astype(jnp.float32)
    scale_rows = lax.rsqrt(jnp.mean(x * x, axis=-1, keepdims=True) + EPSILON)
    normed_input = (x * scale_rows * attention_norm_gain.astype(jnp.float32)).astype(jnp.bfloat16)
    ends = jnp.cumsum(lengths)
    starts = ends - lengths
    token = page_index * token_device_rows + jnp.arange(token_device_rows, dtype=jnp.int32)
    member = (token[:, None] >= starts[None, :]) & (token[:, None] < ends[None, :])
    tok_start = jnp.sum(jnp.where(member, starts[None, :], 0), axis=1)
    tok_adapter = jnp.sum(jnp.where(member, prompt_adapter_index[None, :], 0), axis=1)
    token_position = token - tok_start
    q_cols = wq.shape[1]
    base_query = jnp.dot(
        normed_input,
        lax.all_gather(wq, "page", axis=0, tiled=True),
        preferred_element_type=jnp.float32,
    )
    shrink_all, expand_every_token = (
        lax.all_gather(adapter_down_weight, "page", axis=1, tiled=True),
        lax.all_gather(adapter_up_weight, "page", axis=0, tiled=True),
    )
    adapter_count = shrink_all.shape[1] // ADAPTER_RANK
    feature_number = adapter_down_weight.shape[0]
    own_features = lax.dynamic_slice_in_dim(
        normed_input, head_index * feature_number, feature_number, 1
    )
    partial_every_token = jnp.dot(own_features, shrink_all, preferred_element_type=jnp.float32)
    partial_every_token = partial_every_token.reshape(
        token_device_rows, adapter_count, ADAPTER_RANK
    )
    pick = tok_adapter[:, None] == jnp.arange(adapter_count, dtype=jnp.int32)[None, :]
    partial_sum = jnp.sum(jnp.where(pick[:, :, None], partial_every_token, 0.0), axis=1)
    shrunk = lax.psum(partial_sum, "head").astype(jnp.bfloat16)
    spread_heads = jnp.where(pick[:, :, None], shrunk[:, None, :], jnp.zeros((), jnp.bfloat16))
    spread_heads = spread_heads.reshape(token_device_rows, adapter_count * ADAPTER_RANK)
    adapter_delta = jnp.dot(spread_heads, expand_every_token, preferred_element_type=jnp.float32)
    local_head_count = q_cols // HEAD_WIDTH
    queries = apply_rotation(
        (base_query + adapter_delta).reshape(token_device_rows, local_head_count, HEAD_WIDTH),
        token_position,
        HEAD_WIDTH,
    ).astype(jnp.bfloat16)
    kv_width = key_value_cache.shape[2]
    kv_heads = kv_width // HEAD_WIDTH
    page_count = logical_page_table.shape[1]
    paged = key_value_cache.reshape(page_count, token_device_rows // page_count, 2, kv_width)
    own_block = jnp.take(paged, logical_page_table[0], axis=0).reshape(
        token_device_rows, 2, kv_width
    )

    def pass_on(moving, unused):
        moved = from_behind(moving, "page", 1)
        return (moved, moved)

    unused_last, earlier = lax.scan(pass_on, own_block, None, length=span_count)
    stacked = jnp.concatenate([earlier[::-1], own_block[None]], axis=0)
    block_count = span_count + 1
    key_total = block_count * token_device_rows
    key_index = (page_index - span_count) * token_device_rows + jnp.arange(
        key_total, dtype=jnp.int32
    )
    visible = (key_index[None, :] >= tok_start[:, None]) & (key_index[None, :] <= token[:, None])
    inv_scale = 1.0 / math.sqrt(HEAD_WIDTH)
    group = local_head_count // kv_heads
    outputs = []
    key_stack = stacked[:, :, 0, 0:HEAD_WIDTH]
    value_stack = stacked[:, :, 1, 0:HEAD_WIDTH]
    for member_head in range(group):
        query = queries[:, member_head]
        keys_joined = key_stack.reshape(key_total, HEAD_WIDTH)
        values_joined = value_stack.reshape(key_total, HEAD_WIDTH)
        weights = normalize(score_block(query, keys_joined), visible, inv_scale)
        outputs.append(mix_block(weights, values_joined))
    attended = jnp.stack(outputs, axis=1).reshape(token_device_rows, q_cols).astype(jnp.bfloat16)
    return (queries.reshape(token_device_rows, q_cols), attended)


def solution(mesh):
    return jax.shard_map(
        body,
        mesh=mesh,
        in_specs=(
            P("page", None),
            P(),
            P("page", "head"),
            P("head", "page"),
            P("page", "head"),
            P("page", None, "head"),
            P("page", None),
            P(),
            P(),
        ),
        out_specs=(P("page", "head"), P("page", "head")),
        check_vma=False,
    )
```

profile of v0, /device:TPU:24, one launch (start us, length us, event | category | flops | bytes accessed | tf_op | source)
XLA Modules:
  0.0 495.0 jit_solution(18355755087890017572)
XLA Ops:
  11.2 1.0 copy.54
  13.1 0.7 copy.48
  14.7 0.7 select_reduce_fusion.1
  16.8 2.6 fusion.8
  20.7 157.2 %while.12 = (s32[]{:T(128)}, bf16[384,2,128]{2,1,0:T(2,128)(2,1)S(1)}, bf16[16,384,2,128]{3,1,0,2:T(8,128)(2,1)}, s32[]{:T(128)}) while((s32[]{:T(128)}, bf16[384,2,128]{2,1,0:T(2,128)(2,1)S(1)}, bf16[16,384,2,128]{3,1,0,2:T(8,128)(2,1)}, s32[]{:T(128)}) %tuple.37), condition=%wide.region_7.8_spmd, body=%wide.region_6.7_spmd.sunk | while | flops 2 | bytes 1572969 | solution.py:120
  20.8 3.8 collective-permute-start
  24.6 4.1 collective-permute-done
  29.6 4.4 collective-permute-start
  34.0 3.3 collective-permute-done
  38.1 4.4 collective-permute-start
  42.5 3.2 collective-permute-done
  46.6 4.4 collective-permute-start
  51.0 3.2 collective-permute-done
  55.0 5.3 %collective-permute-start = (bf16[384,2,128]{2,1,0:T(2,128)(2,1)S(1)}, bf16[384,2,128]{2,1,0:T(2,128)(2,1)S(1)}, u32[]{:S(2)}, u32[]{:S(2)}) collective-permute-start(bf16[384,2,128]{2,1,0:T(2,128)(2,1)S(1)} %get-tuple-element.82), channel_id=1, source_target_pairs={{0,8},{8,16},{16,24},{24,32},{32,40},{40,48},{48,56},{56,64},{64,7... | collective-permute-start | bytes 589832 | tf_op jit(solution)/shard_map/while/body/eval_jaxpr/ppermute | solution.py:19
  60.3 3.2 collective-permute-done
  64.4 5.6 %collective-permute-start = (bf16[384,2,128]{2,1,0:T(2,128)(2,1)S(1)}, bf16[384,2,128]{2,1,0:T(2,128)(2,1)S(1)}, u32[]{:S(2)}, u32[]{:S(2)}) collective-permute-start(bf16[384,2,128]{2,1,0:T(2,128)(2,1)S(1)} %get-tuple-element.82), channel_id=1, source_target_pairs={{0,8},{8,16},{16,24},{24,32},{32,40},{40,48},{48,56},{56,64},{64,7... | collective-permute-start | bytes 589832 | tf_op jit(solution)/shard_map/while/body/eval_jaxpr/ppermute | solution.py:19
  69.9 3.2 collective-permute-done
  73.1 0.7 copy_dynamic-update-slice_fusion.2
  74.0 5.6 %collective-permute-start = (bf16[384,2,128]{2,1,0:T(2,128)(2,1)S(1)}, bf16[384,2,128]{2,1,0:T(2,128)(2,1)S(1)}, u32[]{:S(2)}, u32[]{:S(2)}) collective-permute-start(bf16[384,2,128]{2,1,0:T(2,128)(2,1)S(1)} %get-tuple-element.82), channel_id=1, source_target_pairs={{0,8},{8,16},{16,24},{24,32},{32,40},{40,48},{48,56},{56,64},{64,7... | collective-permute-start | bytes 589832 | tf_op jit(solution)/shard_map/while/body/eval_jaxpr/ppermute | solution.py:19
  79.6 3.2 collective-permute-done
  83.7 5.8 %collective-permute-start = (bf16[384,2,128]{2,1,0:T(2,128)(2,1)S(1)}, bf16[384,2,128]{2,1,0:T(2,128)(2,1)S(1)}, u32[]{:S(2)}, u32[]{:S(2)}) collective-permute-start(bf16[384,2,128]{2,1,0:T(2,128)(2,1)S(1)} %get-tuple-element.82), channel_id=1, source_target_pairs={{0,8},{8,16},{16,24},{24,32},{32,40},{40,48},{48,56},{56,64},{64,7... | collective-permute-start | bytes 589832 | tf_op jit(solution)/shard_map/while/body/eval_jaxpr/ppermute | solution.py:19
  89.5 4.1 collective-permute-done
  93.6 0.7 copy_dynamic-update-slice_fusion.2
  94.5 6.2 %collective-permute-start = (bf16[384,2,128]{2,1,0:T(2,128)(2,1)S(1)}, bf16[384,2,128]{2,1,0:T(2,128)(2,1)S(1)}, u32[]{:S(2)}, u32[]{:S(2)}) collective-permute-start(bf16[384,2,128]{2,1,0:T(2,128)(2,1)S(1)} %get-tuple-element.82), channel_id=1, source_target_pairs={{0,8},{8,16},{16,24},{24,32},{32,40},{40,48},{48,56},{56,64},{64,7... | collective-permute-start | bytes 589832 | tf_op jit(solution)/shard_map/while/body/eval_jaxpr/ppermute | solution.py:19
  100.7 5.5 %collective-permute-done = bf16[384,2,128]{2,1,0:T(2,128)(2,1)S(1)} collective-permute-done((bf16[384,2,128]{2,1,0:T(2,128)(2,1)S(1)}, bf16[384,2,128]{2,1,0:T(2,128)(2,1)S(1)}, u32[]{:S(2)}, u32[]{:S(2)}) %collective-permute-start) | collective-permute-done | bytes 196640 | tf_op jit(solution)/shard_map/while/body/eval_jaxpr/ppermute | solution.py:19
  107.1 6.4 %collective-permute-start = (bf16[384,2,128]{2,1,0:T(2,128)(2,1)S(1)}, bf16[384,2,128]{2,1,0:T(2,128)(2,1)S(1)}, u32[]{:S(2)}, u32[]{:S(2)}) collective-permute-start(bf16[384,2,128]{2,1,0:T(2,128)(2,1)S(1)} %get-tuple-element.82), channel_id=1, source_target_pairs={{0,8},{8,16},{16,24},{24,32},{32,40},{40,48},{48,56},{56,64},{64,7... | collective-permute-start | bytes 589832 | tf_op jit(solution)/shard_map/while/body/eval_jaxpr/ppermute | solution.py:19
  113.5 4.9 collective-permute-done
  119.3 5.4 %collective-permute-start = (bf16[384,2,128]{2,1,0:T(2,128)(2,1)S(1)}, bf16[384,2,128]{2,1,0:T(2,128)(2,1)S(1)}, u32[]{:S(2)}, u32[]{:S(2)}) collective-permute-start(bf16[384,2,128]{2,1,0:T(2,128)(2,1)S(1)} %get-tuple-element.82), channel_id=1, source_target_pairs={{0,8},{8,16},{16,24},{24,32},{32,40},{40,48},{48,56},{56,64},{64,7... | collective-permute-start | bytes 589832 | tf_op jit(solution)/shard_map/while/body/eval_jaxpr/ppermute | solution.py:19
  124.7 3.5 collective-permute-done
  129.1 5.9 %collective-permute-start = (bf16[384,2,128]{2,1,0:T(2,128)(2,1)S(1)}, bf16[384,2,128]{2,1,0:T(2,128)(2,1)S(1)}, u32[]{:S(2)}, u32[]{:S(2)}) collective-permute-start(bf16[384,2,128]{2,1,0:T(2,128)(2,1)S(1)} %get-tuple-element.82), channel_id=1, source_target_pairs={{0,8},{8,16},{16,24},{24,32},{32,40},{40,48},{48,56},{56,64},{64,7... | collective-permute-start | bytes 589832 | tf_op jit(solution)/shard_map/while/body/eval_jaxpr/ppermute | solution.py:19
  135.0 3.3 collective-permute-done
  139.1 5.6 %collective-permute-start = (bf16[384,2,128]{2,1,0:T(2,128)(2,1)S(1)}, bf16[384,2,128]{2,1,0:T(2,128)(2,1)S(1)}, u32[]{:S(2)}, u32[]{:S(2)}) collective-permute-start(bf16[384,2,128]{2,1,0:T(2,128)(2,1)S(1)} %get-tuple-element.82), channel_id=1, source_target_pairs={{0,8},{8,16},{16,24},{24,32},{32,40},{40,48},{48,56},{56,64},{64,7... | collective-permute-start | bytes 589832 | tf_op jit(solution)/shard_map/while/body/eval_jaxpr/ppermute | solution.py:19
  144.7 3.3 collective-permute-done
  148.9 5.7 %collective-permute-start = (bf16[384,2,128]{2,1,0:T(2,128)(2,1)S(1)}, bf16[384,2,128]{2,1,0:T(2,128)(2,1)S(1)}, u32[]{:S(2)}, u32[]{:S(2)}) collective-permute-start(bf16[384,2,128]{2,1,0:T(2,128)(2,1)S(1)} %get-tuple-element.82), channel_id=1, source_target_pairs={{0,8},{8,16},{16,24},{24,32},{32,40},{40,48},{48,56},{56,64},{64,7... | collective-permute-start | bytes 589832 | tf_op jit(solution)/shard_map/while/body/eval_jaxpr/ppermute | solution.py:19
  154.6 3.2 collective-permute-done
  158.6 5.4 %collective-permute-start = (bf16[384,2,128]{2,1,0:T(2,128)(2,1)S(1)}, bf16[384,2,128]{2,1,0:T(2,128)(2,1)S(1)}, u32[]{:S(2)}, u32[]{:S(2)}) collective-permute-start(bf16[384,2,128]{2,1,0:T(2,128)(2,1)S(1)} %get-tuple-element.82), channel_id=1, source_target_pairs={{0,8},{8,16},{16,24},{24,32},{32,40},{40,48},{48,56},{56,64},{64,7... | collective-permute-start | bytes 589832 | tf_op jit(solution)/shard_map/while/body/eval_jaxpr/ppermute | solution.py:19
  164.0 3.2 collective-permute-done
  168.0 5.6 %collective-permute-start = (bf16[384,2,128]{2,1,0:T(2,128)(2,1)S(1)}, bf16[384,2,128]{2,1,0:T(2,128)(2,1)S(1)}, u32[]{:S(2)}, u32[]{:S(2)}) collective-permute-start(bf16[384,2,128]{2,1,0:T(2,128)(2,1)S(1)} %get-tuple-element.82), channel_id=1, source_target_pairs={{0,8},{8,16},{16,24},{24,32},{32,40},{40,48},{48,56},{56,64},{64,7... | collective-permute-start | bytes 589832 | tf_op jit(solution)/shard_map/while/body/eval_jaxpr/ppermute | solution.py:19
  173.6 3.5 collective-permute-done
  177.1 0.7 copy_dynamic-update-slice_fusion.2
  177.9 4.1 rev.3
  182.6 1.1 multiply_cosine_fusion
  183.7 3.9 fusion.15
  187.6 3.4 fusion.10
  191.0 2.1 fusion.24
  193.4 20.0 %psum.7 = bf16[384,16]{0,1:T(8,128)(2,1)S(1)} all-reduce(f32[384,16]{0,1:T(8,128)S(1)} %select_reduce_fusion), channel_id=1, replica_groups=mesh['page'=64,'head'=8] {'head'}, use_global_device_ids=true, to_apply=%region_4.5 | all-reduce | flops 6144 | bytes 36864 | tf_op jit(solution)/shard_map/psum | solution.py:98
  213.6 86.4 %all-gather.4.cloned.1.call-done = bf16[4096,512]{1,0:T(8,128)(2,1)} async-done(((bf16[64,512]{1,0:T(8,128)(2,1)}), bf16[4096,512]{1,0:T(8,128)(2,1)}) %all-gather.4.cloned.1.call-update) | async-done | bytes 4194320 | tf_op jit(solution)/shard_map/all_gather | solution.py:80
  299.9 5.8 %fusion.32 = f32[384,512]{1,0:T(8,128)} fusion(bf16[384,4096]{1,0:T(8,128)(2,1)} %fusion.10, bf16[4096,512]{1,0:T(8,128)(2,1)} %all-gather.4.cloned.1.call-done), kind=kOutput, calls=%fused_computation.81 | convolution fusion | flops 1610612736 | bytes 8126464 | tf_op jit(solution)/shard_map/dot_general | solution.py:78
  305.8 130.7 %all-gather.8.cloned.1.call-done = bf16[1024,512]{1,0:T(8,128)(2,1)} async-done(((bf16[16,512]{1,0:T(8,128)(2,1)}), bf16[1024,512]{1,0:T(8,128)(2,1)}) %all-gather.8.cloned.1.call-update) | async-done | bytes 1048592 | tf_op jit(solution)/shard_map/all_gather | solution.py:85
  436.5 2.0 convolution_add_fusion
  439.0 5.4 %fusion.31 = (f32[384]{0:T(512)S(1)}, f32[384,6528]{1,0:T(8,128)}) fusion(bf16[6528,128]{1,0:T(8,128)(2,1)S(1)} %bitcast.78, bf16[384,4,128]{0,2,1:T(8,128)(2,1)S(1)} %maximum_convert_fusion, s32[384]{0:T(512)S(1)} %copy-done.6, s32[384]{0:T(512)S(1)} %copy-done.8, s32[6528]{0:T(1024)S(1)} %copy-done.4), kind=kOutput, calls=%fused_computation.80 | convolution fusion | flops 656768640 | bytes 11830784 | tf_op jit(solution)/shard_map/dot_general | solution.py:36
  444.4 5.5 %fusion.30 = (f32[384]{0:T(512)S(1)}, f32[384,6528]{1,0:T(8,128)}) fusion(bf16[6528,128]{1,0:T(8,128)(2,1)S(1)} %bitcast.79, bf16[384,4,128]{0,2,1:T(8,128)(2,1)S(1)} %maximum_convert_fusion, s32[384]{0:T(512)S(1)} %copy-done.6, s32[384]{0:T(512)S(1)} %copy-done.8, s32[6528]{0:T(1024)S(1)} %copy-done.4), kind=kOutput, calls=%fused_computation.79 | convolution fusion | flops 656768640 | bytes 11830784 | tf_op jit(solution)/shard_map/dot_general | solution.py:36
  449.9 3.0 fusion.29
  452.9 3.0 fusion.28
  455.8 5.4 %fusion.4 = f32[384]{0:T(512)S(1)} fusion(f32[384,6528]{1,0:T(8,128)} %get-tuple-element.57, f32[384]{0:T(512)S(1)} %get-tuple-element.56), kind=kLoop, calls=%fused_computation.19 | loop fusion | flops 5013120 | bytes 10030080 | tf_op jit(solution)/shard_map/reduce_sum | solution.py:49
  461.3 6.1 %fusion.20 = bf16[384,1,128]{0,2,1:T(8,128)(2,1)S(1)} fusion(bf16[6528,128]{1,0:T(8,128)(2,1)S(1)} %bitcast.74, f32[384,6528]{1,0:T(8,128)} %get-tuple-element.57, f32[384]{0:T(512)S(1)} %fusion.4, f32[384]{0:T(512)S(1)} %get-tuple-element.56), kind=kOutput, calls=%fused_computation.42 | convolution fusion | flops 649297920 | bytes 11799552 | tf_op jit(solution)/shard_map/dot_general | solution.py:42
  467.4 5.3 %fusion.5 = f32[384]{0:T(512)S(1)} fusion(f32[384,6528]{1,0:T(8,128)} %get-tuple-element.55, f32[384]{0:T(512)S(1)} %get-tuple-element.54), kind=kLoop, calls=%fused_computation.20 | loop fusion | flops 5013120 | bytes 10030080 | tf_op jit(solution)/shard_map/reduce_sum | solution.py:49
  472.7 6.3 %fusion.21 = bf16[384,1,128]{0,2,1:T(8,128)(2,1)S(1)} fusion(bf16[6528,128]{1,0:T(8,128)(2,1)S(1)} %bitcast.75, f32[384,6528]{1,0:T(8,128)} %get-tuple-element.55, f32[384]{0:T(512)S(1)} %fusion.5, f32[384]{0:T(512)S(1)} %get-tuple-element.54), kind=kOutput, calls=%fused_computation.43 | convolution fusion | flops 649297920 | bytes 11799552 | tf_op jit(solution)/shard_map/dot_general | solution.py:42
  479.0 1.5 fusion.6
  480.5 2.2 fusion.22
  482.8 1.5 fusion.7
  484.3 2.2 fusion.23
  486.6 0.9 copy.64
  487.5 0.9 copy.63
  (80 shorter events, 21.3 us)
Async XLA Ops:
  7.2 183.8 %all-gather.6.cloned.1.call-start = ((), (), s32[]{:S(2)}) async-start(), calls=%async_computation.1 | async-start | bytes 1064960 | tf_op jit(solution)/shard_map/all_gather | solution.py:84
  7.9 292.0 %all-gather.4.cloned.1.call-start = ((), (), s32[]{:S(2)}) async-start(), calls=%async_computation | async-start | bytes 4259840 | tf_op jit(solution)/shard_map/all_gather | solution.py:80
  8.6 427.9 %all-gather.8.cloned.1.call-start = ((), (), s32[]{:S(2)}) async-start(), calls=%async_computation.2 | async-start | bytes 1064960 | tf_op jit(solution)/shard_map/all_gather | solution.py:85
  13.1 6.8 %copy-start.5 = (s32[384]{0:T(512)}, s32[384]{0:T(512)S(1)}, u32[]{:S(2)}) copy-start(s32[384]{0:T(512)S(1)} %iota_add_fusion.1) | copy-start | bytes 4612
  15.4 4.5 copy-start.7
  20.8 8.0 %collective-permute-start = (bf16[384,2,128]{2,1,0:T(2,128)(2,1)S(1)}, bf16[384,2,128]{2,1,0:T(2,128)(2,1)S(1)}, u32[]{:S(2)}, u32[]{:S(2)}) collective-permute-start(bf16[384,2,128]{2,1,0:T(2,128)(2,1)S(1)} %get-tuple-element.82), channel_id=1, source_target_pairs={{0,8},{8,16},{16,24},{24,32},{32,40},{40,48},{48,56},{56,64},{64,7... | collective-permute-start | bytes 589832 | tf_op jit(solution)/shard_map/while/body/eval_jaxpr/ppermute | solution.py:19
  29.6 7.7 %collective-permute-start = (bf16[384,2,128]{2,1,0:T(2,128)(2,1)S(1)}, bf16[384,2,128]{2,1,0:T(2,128)(2,1)S(1)}, u32[]{:S(2)}, u32[]{:S(2)}) collective-permute-start(bf16[384,2,128]{2,1,0:T(2,128)(2,1)S(1)} %get-tuple-element.82), channel_id=1, source_target_pairs={{0,8},{8,16},{16,24},{24,32},{32,40},{40,48},{48,56},{56,64},{64,7... | collective-permute-start | bytes 589832 | tf_op jit(solution)/shard_map/while/body/eval_jaxpr/ppermute | solution.py:19
  38.1 7.6 %collective-permute-start = (bf16[384,2,128]{2,1,0:T(2,128)(2,1)S(1)}, bf16[384,2,128]{2,1,0:T(2,128)(2,1)S(1)}, u32[]{:S(2)}, u32[]{:S(2)}) collective-permute-start(bf16[384,2,128]{2,1,0:T(2,128)(2,1)S(1)} %get-tuple-element.82), channel_id=1, source_target_pairs={{0,8},{8,16},{16,24},{24,32},{32,40},{40,48},{48,56},{56,64},{64,7... | collective-permute-start | bytes 589832 | tf_op jit(solution)/shard_map/while/body/eval_jaxpr/ppermute | solution.py:19
  46.6 7.6 %collective-permute-start = (bf16[384,2,128]{2,1,0:T(2,128)(2,1)S(1)}, bf16[384,2,128]{2,1,0:T(2,128)(2,1)S(1)}, u32[]{:S(2)}, u32[]{:S(2)}) collective-permute-start(bf16[384,2,128]{2,1,0:T(2,128)(2,1)S(1)} %get-tuple-element.82), channel_id=1, source_target_pairs={{0,8},{8,16},{16,24},{24,32},{32,40},{40,48},{48,56},{56,64},{64,7... | collective-permute-start | bytes 589832 | tf_op jit(solution)/shard_map/while/body/eval_jaxpr/ppermute | solution.py:19
  55.0 8.5 %collective-permute-start = (bf16[384,2,128]{2,1,0:T(2,128)(2,1)S(1)}, bf16[384,2,128]{2,1,0:T(2,128)(2,1)S(1)}, u32[]{:S(2)}, u32[]{:S(2)}) collective-permute-start(bf16[384,2,128]{2,1,0:T(2,128)(2,1)S(1)} %get-tuple-element.82), channel_id=1, source_target_pairs={{0,8},{8,16},{16,24},{24,32},{32,40},{40,48},{48,56},{56,64},{64,7... | collective-permute-start | bytes 589832 | tf_op jit(solution)/shard_map/while/body/eval_jaxpr/ppermute | solution.py:19
  64.4 8.8 %collective-permute-start = (bf16[384,2,128]{2,1,0:T(2,128)(2,1)S(1)}, bf16[384,2,128]{2,1,0:T(2,128)(2,1)S(1)}, u32[]{:S(2)}, u32[]{:S(2)}) collective-permute-start(bf16[384,2,128]{2,1,0:T(2,128)(2,1)S(1)} %get-tuple-element.82), channel_id=1, source_target_pairs={{0,8},{8,16},{16,24},{24,32},{32,40},{40,48},{48,56},{56,64},{64,7... | collective-permute-start | bytes 589832 | tf_op jit(solution)/shard_map/while/body/eval_jaxpr/ppermute | solution.py:19
  74.0 8.8 %collective-permute-start = (bf16[384,2,128]{2,1,0:T(2,128)(2,1)S(1)}, bf16[384,2,128]{2,1,0:T(2,128)(2,1)S(1)}, u32[]{:S(2)}, u32[]{:S(2)}) collective-permute-start(bf16[384,2,128]{2,1,0:T(2,128)(2,1)S(1)} %get-tuple-element.82), channel_id=1, source_target_pairs={{0,8},{8,16},{16,24},{24,32},{32,40},{40,48},{48,56},{56,64},{64,7... | collective-permute-start | bytes 589832 | tf_op jit(solution)/shard_map/while/body/eval_jaxpr/ppermute | solution.py:19
  83.7 9.9 %collective-permute-start = (bf16[384,2,128]{2,1,0:T(2,128)(2,1)S(1)}, bf16[384,2,128]{2,1,0:T(2,128)(2,1)S(1)}, u32[]{:S(2)}, u32[]{:S(2)}) collective-permute-start(bf16[384,2,128]{2,1,0:T(2,128)(2,1)S(1)} %get-tuple-element.82), channel_id=1, source_target_pairs={{0,8},{8,16},{16,24},{24,32},{32,40},{40,48},{48,56},{56,64},{64,7... | collective-permute-start | bytes 589832 | tf_op jit(solution)/shard_map/while/body/eval_jaxpr/ppermute | solution.py:19
  94.5 11.8 %collective-permute-start = (bf16[384,2,128]{2,1,0:T(2,128)(2,1)S(1)}, bf16[384,2,128]{2,1,0:T(2,128)(2,1)S(1)}, u32[]{:S(2)}, u32[]{:S(2)}) collective-permute-start(bf16[384,2,128]{2,1,0:T(2,128)(2,1)S(1)} %get-tuple-element.82), channel_id=1, source_target_pairs={{0,8},{8,16},{16,24},{24,32},{32,40},{40,48},{48,56},{56,64},{64,7... | collective-permute-start | bytes 589832 | tf_op jit(solution)/shard_map/while/body/eval_jaxpr/ppermute | solution.py:19
  107.1 11.3 %collective-permute-start = (bf16[384,2,128]{2,1,0:T(2,128)(2,1)S(1)}, bf16[384,2,128]{2,1,0:T(2,128)(2,1)S(1)}, u32[]{:S(2)}, u32[]{:S(2)}) collective-permute-start(bf16[384,2,128]{2,1,0:T(2,128)(2,1)S(1)} %get-tuple-element.82), channel_id=1, source_target_pairs={{0,8},{8,16},{16,24},{24,32},{32,40},{40,48},{48,56},{56,64},{64,7... | collective-permute-start | bytes 589832 | tf_op jit(solution)/shard_map/while/body/eval_jaxpr/ppermute | solution.py:19
  119.3 8.9 %collective-permute-start = (bf16[384,2,128]{2,1,0:T(2,128)(2,1)S(1)}, bf16[384,2,128]{2,1,0:T(2,128)(2,1)S(1)}, u32[]{:S(2)}, u32[]{:S(2)}) collective-permute-start(bf16[384,2,128]{2,1,0:T(2,128)(2,1)S(1)} %get-tuple-element.82), channel_id=1, source_target_pairs={{0,8},{8,16},{16,24},{24,32},{32,40},{40,48},{48,56},{56,64},{64,7... | collective-permute-start | bytes 589832 | tf_op jit(solution)/shard_map/while/body/eval_jaxpr/ppermute | solution.py:19
  129.1 9.2 %collective-permute-start = (bf16[384,2,128]{2,1,0:T(2,128)(2,1)S(1)}, bf16[384,2,128]{2,1,0:T(2,128)(2,1)S(1)}, u32[]{:S(2)}, u32[]{:S(2)}) collective-permute-start(bf16[384,2,128]{2,1,0:T(2,128)(2,1)S(1)} %get-tuple-element.82), channel_id=1, source_target_pairs={{0,8},{8,16},{16,24},{24,32},{32,40},{40,48},{48,56},{56,64},{64,7... | collective-permute-start | bytes 589832 | tf_op jit(solution)/shard_map/while/body/eval_jaxpr/ppermute | solution.py:19
  139.1 8.9 %collective-permute-start = (bf16[384,2,128]{2,1,0:T(2,128)(2,1)S(1)}, bf16[384,2,128]{2,1,0:T(2,128)(2,1)S(1)}, u32[]{:S(2)}, u32[]{:S(2)}) collective-permute-start(bf16[384,2,128]{2,1,0:T(2,128)(2,1)S(1)} %get-tuple-element.82), channel_id=1, source_target_pairs={{0,8},{8,16},{16,24},{24,32},{32,40},{40,48},{48,56},{56,64},{64,7... | collective-permute-start | bytes 589832 | tf_op jit(solution)/shard_map/while/body/eval_jaxpr/ppermute | solution.py:19
  148.9 8.9 %collective-permute-start = (bf16[384,2,128]{2,1,0:T(2,128)(2,1)S(1)}, bf16[384,2,128]{2,1,0:T(2,128)(2,1)S(1)}, u32[]{:S(2)}, u32[]{:S(2)}) collective-permute-start(bf16[384,2,128]{2,1,0:T(2,128)(2,1)S(1)} %get-tuple-element.82), channel_id=1, source_target_pairs={{0,8},{8,16},{16,24},{24,32},{32,40},{40,48},{48,56},{56,64},{64,7... | collective-permute-start | bytes 589832 | tf_op jit(solution)/shard_map/while/body/eval_jaxpr/ppermute | solution.py:19
  158.6 8.6 %collective-permute-start = (bf16[384,2,128]{2,1,0:T(2,128)(2,1)S(1)}, bf16[384,2,128]{2,1,0:T(2,128)(2,1)S(1)}, u32[]{:S(2)}, u32[]{:S(2)}) collective-permute-start(bf16[384,2,128]{2,1,0:T(2,128)(2,1)S(1)} %get-tuple-element.82), channel_id=1, source_target_pairs={{0,8},{8,16},{16,24},{24,32},{32,40},{40,48},{48,56},{56,64},{64,7... | collective-permute-start | bytes 589832 | tf_op jit(solution)/shard_map/while/body/eval_jaxpr/ppermute | solution.py:19
  168.0 9.0 %collective-permute-start = (bf16[384,2,128]{2,1,0:T(2,128)(2,1)S(1)}, bf16[384,2,128]{2,1,0:T(2,128)(2,1)S(1)}, u32[]{:S(2)}, u32[]{:S(2)}) collective-permute-start(bf16[384,2,128]{2,1,0:T(2,128)(2,1)S(1)} %get-tuple-element.82), channel_id=1, source_target_pairs={{0,8},{8,16},{16,24},{24,32},{32,40},{40,48},{48,56},{56,64},{64,7... | collective-permute-start | bytes 589832 | tf_op jit(solution)/shard_map/while/body/eval_jaxpr/ppermute | solution.py:19
  177.9 9.7 %copy-start = (bf16[384,4096]{1,0:T(8,128)(2,1)S(1)}, bf16[384,4096]{1,0:T(8,128)(2,1)}, u32[]{:S(2)}) copy-start(bf16[384,4096]{1,0:T(8,128)(2,1)} %param.11) | copy-start | bytes 9437188
  187.6 5.5 %copy-start.3 = (pred[384,64]{0,1:T(8,128)(4,1)S(1)}, pred[384,64]{0,1:T(8,128)(4,1)}, u32[]{:S(2)}) copy-start(pred[384,64]{0,1:T(8,128)(4,1)} %iota_compare_fusion) | copy-start | bytes 73732
  305.7 133.2 %copy-start.2 = (bf16[17,384,1,128]{3,1,0,2:T(8,128)(2,1)S(1)}, bf16[17,384,1,128]{3,1,0,2:T(8,128)(2,1)}, u32[]{:S(2)}) copy-start(bf16[17,384,1,128]{3,1,0,2:T(8,128)(2,1)} %get-tuple-element.44) | copy-start | bytes 5013508
  305.8 133.2 %copy-start.4 = (s32[6528]{0:T(1024)S(1)}, s32[6528]{0:T(1024)}, u32[]{:S(2)}) copy-start(s32[6528]{0:T(1024)} %iota_add_fusion) | copy-start | bytes 78340
  305.8 133.3 %copy-start.6 = (s32[384]{0:T(512)S(1)}, s32[384]{0:T(512)}, u32[]{:S(2)}) copy-start(s32[384]{0:T(512)} %copy-done.5) | copy-start | bytes 4612
  305.8 133.3 %copy-start.8 = (s32[384]{0:T(512)S(1)}, s32[384]{0:T(512)}, u32[]{:S(2)}) copy-start(s32[384]{0:T(512)} %copy-done.7) | copy-start | bytes 4612
  455.8 5.4 %copy-start.1 = (bf16[17,384,1,128]{3,1,0,2:T(8,128)(2,1)S(1)}, bf16[17,384,1,128]{3,1,0,2:T(8,128)(2,1)}, u32[]{:S(2)}) copy-start(bf16[17,384,1,128]{3,1,0,2:T(8,128)(2,1)} %get-tuple-element.45) | copy-start | bytes 5013508
Sparse Core Ops, SparseCore 0:
  10.9 143.6 all-gather.5
  157.6 142.3 all-gather.3
  302.9 133.5 all-gather.7
where the time goes:
time: 496 us; the launch traced here: 495 us
  waiting for transfers between devices  277 us (56%)
  starting transfers between devices  85.5 us (17%)
  matrix products  43.5 us (9%)
  other arithmetic  32.2 us (6%)
  local copies, waits for them, and re-layouts  22.2 us (4%)
  blocking collectives  20 us (4%)
  between operations  14 us (3%)
    all_gather x1, waiting for transfers between devices, body(): lax.all_gather(adapter_up_weight, 'page', axis=0, tiled=True)  131 us
    all_gather x1, waiting for transfers between devices, body(): lax.all_gather(wq, 'page', axis=0, tiled=True)  86.4 us
    ppermute x16, starting transfers between devices, from_behind(): lax.ppermute(value, axis, [(source, source + steps) for source in range(l...  85.4 us
    ppermute x16, waiting for transfers between devices, from_behind(): lax.ppermute(value, axis, [(source, source + steps) for source in range(l...  57.9 us
    psum x1, blocking collectives, body(): shrunk = lax.psum(partial_sum, 'head').astype(jnp.bfloat16)  20 us
    dot_general x4, matrix products, score_block(): lax.dot_general(query, keyblock, (((1,), (1,)), ((), ())), preferred_elem...  16.8 us
    dot_general x4, matrix products, mix_block(): return jnp.dot(weights, valueblock, preferred_element_type=jnp.float32)  16.8 us
    reduce_sum x4, other arithmetic, normalize(): return (expo / jnp.sum(expo, axis=-1, keepdims=True)).astype(jnp.bfloat16)  13.9 us
  transfers between devices with their start and end apart: 19, of which 18 were waited for; matrix products, arithmetic and copies ran while one was open for 9% of the time, Pallas kernels for 0%

commit v1 on v0

v1 whole, which is shorter than its diff:
```python
import functools
import math

import jax
import jax.numpy as jnp
from jax import lax
from jax.experimental import pallas as pl
from jax.experimental.pallas import tpu as pltpu
from jax.sharding import PartitionSpec as P

HEAD_WIDTH = 128
RANK = 16
EPSILON = 1e-05
ROPE_BASE = 500000.0
NX = 4
MASKED = -1e30
LAG_NEAR = 2
LAG_FAR = 4


def clamp(value, low, high):
    return jnp.minimum(jnp.maximum(value, low), high)


def kernel(
    nz,
    nh,
    length_ref,
    prompt_adapter_ref,
    table_ref,
    hidden_ref,
    gain_ref,
    wq_ref,
    down_ref,
    up_ref,
    kv_ref,
    freq_ref,
    query_ref,
    out_ref,
    normed,
    own_feat,
    ga,
    gw,
    kvb,
    acc,
    start_col,
    adapter_col,
    adapter_row,
    cosine,
    sine,
    partial,
    psum,
    scores,
    recv_a,
    recv_w,
    send_za,
    send_zw,
    send_xa,
    send_xw,
    recv_kv,
    send_kf,
    send_kb,
    recv_h,
    send_h,
):
    page_axis = NX * nz
    tokens, width = hidden_ref.shape
    feat = wq_ref.shape[0]
    cols = wq_ref.shape[1]
    heads = cols // HEAD_WIDTH
    own_width = own_feat.shape[1]
    requests = length_ref.shape[0]
    pages = kv_ref.shape[0]
    page_rows = kv_ref.shape[1]
    me = lax.axis_index("page")
    head = lax.axis_index("head")
    x = me // nz
    z = me % nz
    z_up = x * nz + (z + 1) % nz
    z_down = x * nz + (z + nz - 1) % nz
    x_up = ((x + 1) % NX) * nz + z
    x_down = ((x + NX - 1) % NX) * nz + z
    p_up = (me + 1) % page_axis
    p_down = (me + page_axis - 1) % page_axis
    left_x = (x + NX - 1) % NX
    right_x = (x + 1) % NX
    far_x = (x + 2) % NX

    def send(src, dst, send_sem, recv_sem, page):
        return pltpu.make_async_remote_copy(
            src_ref=src,
            dst_ref=dst,
            send_sem=send_sem,
            recv_sem=recv_sem,
            device_id={"page": page},
            device_id_type=pl.DeviceIdType.MESH,
        )

    barrier = pltpu.get_barrier_semaphore()
    for page in (z_up, z_down, x_up, x_down, p_up, p_down):
        pl.semaphore_signal(
            barrier, inc=1, device_id={"page": page}, device_id_type=pl.DeviceIdType.MESH
        )
    for step in range(1, nh):
        pl.semaphore_signal(
            barrier,
            inc=1,
            device_id={"head": (head + step) % nh},
            device_id_type=pl.DeviceIdType.MESH,
        )

    ga[z, x, 0:RANK, :] = up_ref[...]
    ga[z, x, RANK : 2 * RANK, :] = (
        jnp.transpose(down_ref[...].astype(jnp.float32)).astype(jnp.bfloat16)
    )
    gw[z, x] = wq_ref[...]
    for j in range(pages):
        page_block = kv_ref[table_ref[0, j]]
        kvb[0, 0, j * page_rows : (j + 1) * page_rows, :] = page_block[:, :HEAD_WIDTH]
        kvb[0, 1, j * page_rows : (j + 1) * page_rows, :] = page_block[:, HEAD_WIDTH:]
    pl.semaphore_wait(barrier, 6 + nh - 1)

    low = nz // 4
    high = nz - 1 - low

    def reach(offset):
        return clamp(nz - 1 - (z + 2 * nz - offset) % nz, low, high)

    def kv_forward(offset, half):
        return send(
            kvb.at[offset, half],
            kvb.at[offset + 1, half],
            send_kf.at[offset, half],
            recv_kv.at[offset + 1, half],
            p_up,
        )

    def kv_backward(offset, half):
        return send(
            kvb.at[offset, half],
            kvb.at[offset - 1, half],
            send_kb.at[offset, half],
            recv_kv.at[offset - 1, half],
            p_down,
        )

    def kv_cross(half):
        return send(
            kvb.at[0, half],
            kvb.at[nz, half],
            send_kb.at[0, half],
            recv_kv.at[nz, half],
            x_up,
        )

    def kv_wait(offset, half):
        send(
            kvb.at[0, half],
            kvb.at[offset, half],
            send_kb.at[0, half],
            recv_kv.at[offset, half],
            x_up,
        ).wait_recv()

    def kv_step(j):
        reach_up = reach(j)
        back = nz + 1 - j
        reach_back = reach(back)
        for half in range(2):

            @pl.when(j <= reach_up)
            def _():
                kv_wait(j, half)

                @pl.when(j + 1 <= reach_up)
                def _():
                    kv_forward(j, half).start()

            @pl.when(back > reach_back)
            def _():
                kv_wait(back, half)

                @pl.when(back - 1 > reach_back)
                def _():
                    kv_backward(back, half).start()

    def position(i):
        distance = (i + 1) // 2
        return jnp.where(i % 2 == 1, (z + nz - distance) % nz, (z + distance) % nz)

    def weight_stream(buf, recv, send_z, send_x):
        def z_copy(i, zz, page, slot):
            return send(buf.at[zz, x], buf.at[zz, x], send_z.at[slot], recv.at[zz, x], page)

        def x_copy(zz, xx, page, which):
            return send(
                buf.at[zz, xx], buf.at[zz, xx], send_x.at[which, zz], recv.at[zz, xx], page
            )

        def wait(zz, xx):
            send(
                buf.at[zz, xx], buf.at[zz, xx], send_x.at[0, zz], recv.at[zz, xx], x_up
            ).wait_recv()

        def arrive(i):
            zz = position(i)

            @pl.when(i > 0)
            def _():
                wait(zz, x)

            @pl.when(((i % 2 == 1) & ((i + 1) // 2 < nz // 2)) | (i == 0))
            def _():
                z_copy(i, zz, z_up, i).start()

            @pl.when(((i % 2 == 0) & ((i + 1) // 2 < nz // 2 - 1)))
            def _():
                z_copy(i, zz, z_down, jnp.where(i == 0, nz, i)).start()

            x_copy(zz, x, x_up, 0).start()
            x_copy(zz, x, x_down, 1).start()

        def near(i):
            zz = position(i)
            wait(zz, left_x)

            @pl.when(i % 2 == 0)
            def _():
                x_copy(zz, left_x, x_up, 2).start()

            wait(zz, right_x)

            @pl.when(i % 2 == 1)
            def _():
                x_copy(zz, right_x, x_down, 2).start()

        def far(i):
            zz = position(i)
            wait(zz, far_x)
            return zz

        def finish(i):
            zz = position(i)

            @pl.when(((i % 2 == 1) & ((i + 1) // 2 < nz // 2)) | (i == 0))
            def _():
                z_copy(i, zz, z_up, i).wait_send()

            @pl.when(((i % 2 == 0) & ((i + 1) // 2 < nz // 2 - 1)))
            def _():
                z_copy(i, zz, z_down, jnp.where(i == 0, nz, i)).wait_send()

            x_copy(zz, x, x_up, 0).wait_send()
            x_copy(zz, x, x_down, 1).wait_send()
            x_copy(zz, left_x, x_up, 2).wait_send()

        return arrive, near, far, finish

    a_arrive, a_near, a_far, a_finish = weight_stream(ga, recv_a, send_za, send_xa)
    w_arrive, w_near, w_far, w_finish = weight_stream(gw, recv_w, send_zw, send_xw)

    a_arrive(0)
    for half in range(2):

        @pl.when(reach(0) >= 1)
        def _():
            kv_forward(0, half).start()

        kv_cross(half).start()

    def prompts(token):
        start = jnp.zeros(token.shape, jnp.int32)
        adapter = jnp.zeros(token.shape, jnp.int32)
        end = jnp.int32(0)
        for r in range(requests):
            begin = end
            end = end + length_ref[r]
            inside = (token >= begin) & (token < end)
            start = jnp.where(inside, begin, start)
            adapter = jnp.where(inside, prompt_adapter_ref[r], adapter)
        return start, adapter

    token_row = me * tokens + lax.broadcasted_iota(jnp.int32, (8, tokens), 1)
    adapter_row[...] = prompts(token_row)[1]

    rows_step = 32

    def norm_rows(step, carry):
        rows = pl.ds(pl.multiple_of(step * rows_step, rows_step), rows_step)
        value = hidden_ref[rows, :].astype(jnp.float32)
        scale = lax.rsqrt(jnp.mean(value * value, axis=-1, keepdims=True) + EPSILON)
        value = value * scale * gain_ref[...].astype(jnp.float32)
        lane = lax.broadcasted_iota(jnp.int32, (rows_step, 2 * feat), 1)
        lower = lane < feat
        for pair in range(nz // 2):
            piece = [
                value[:, (k * nz // 2 + pair) * 2 * feat : (k * nz // 2 + pair + 1) * 2 * feat]
                for k in range(NX)
            ]
            for k in range(0, NX, 2):
                even = jnp.where(lower, piece[k], pltpu.roll(piece[k + 1], feat, 1))
                odd = jnp.where(lower, pltpu.roll(piece[k], feat, 1), piece[k + 1])
                normed[2 * pair, rows, k * feat : (k + 2) * feat] = even.astype(jnp.bfloat16)
                normed[2 * pair + 1, rows, k * feat : (k + 2) * feat] = odd.astype(jnp.bfloat16)
        mine = pl.ds(pl.multiple_of(head * own_width, own_width), own_width)
        own = hidden_ref[rows, mine].astype(jnp.float32)
        own = own * scale * gain_ref[:, mine].astype(jnp.float32)
        own_feat[rows, :] = own.astype(jnp.bfloat16)
        token = me * tokens + step * rows_step + lax.broadcasted_iota(
            jnp.int32, (rows_step, HEAD_WIDTH), 0
        )
        start, adapter = prompts(token)
        start_col[rows, :] = start
        adapter_col[rows, :] = adapter
        return carry

    lax.fori_loop(0, tokens // rows_step, norm_rows, 0)
    acc[...] = jnp.zeros_like(acc)
    partial[...] = jnp.zeros_like(partial)

    def head_copy(step):
        return pltpu.make_async_remote_copy(
            src_ref=psum.at[0],
            dst_ref=psum.at[step],
            send_sem=send_h.at[step],
            recv_sem=recv_h.at[step],
            device_id={"head": (head + step) % nh},
            device_id_type=pl.DeviceIdType.MESH,
        )

    def stage(n, first, count, body):
        @pl.when((n >= first) & (n < first + count))
        def _():
            body(n - first)

    def a_compute(i):
        zz = a_far(i)
        block = ga[zz, :, RANK : 2 * RANK, :].reshape(NX * RANK, cols)
        part = lax.dot_general(
            block, own_feat[...], (((1,), (1,)), ((), ())), preferred_element_type=jnp.float32
        )
        wanted = adapter_row[...]
        wanted = jnp.concatenate([wanted, wanted], axis=0)
        total = partial[...]
        for k in range(NX):
            total += jnp.where(wanted == k * nz + zz, part[k * RANK : (k + 1) * RANK], 0.0)
        partial[...] = total

        @pl.when(i == nz - 1)
        def _():
            psum[0] = total
            for step in range(1, nh):
                head_copy(step).start()

    def w_compute(i):
        zz = w_far(i)
        acc[...] += jnp.dot(
            normed[zz], gw[zz].reshape(NX * feat, cols), preferred_element_type=jnp.float32
        )

    early = nz // 4

    def weights_step(n, carry):
        stage(n, 1, nz - 1, lambda i: a_arrive(i + 1))
        stage(n, nz, nz, w_arrive)
        stage(n, LAG_NEAR, nz, a_near)
        stage(n, nz + LAG_NEAR, nz, w_near)
        stage(n, LAG_FAR, nz, a_compute)

        @pl.when((n < nz) & (n % 4 == 3))
        def _():
            kv_step((n + 1) // 4)

        stage(n, nz + LAG_FAR, nz, w_compute)

        @pl.when((n >= nz) & (n < 2 * nz) & ((n - nz) % 2 == 1))
        def _():
            kv_step(early + (n - nz + 1) // 2)

        return carry

    lax.fori_loop(0, 2 * nz + LAG_FAR, weights_step, 0)

    def late_step(j, carry):
        kv_step(j)
        return carry

    for step in range(1, nh):
        head_copy(step).wait_recv()
    shrunk = psum[0]
    for step in range(1, nh):
        shrunk = shrunk + psum[step]
    shrunk = shrunk.astype(jnp.bfloat16).astype(jnp.float32)
    shrunk = jnp.concatenate([shrunk] * (HEAD_WIDTH // RANK), axis=0)
    shrunk = jnp.transpose(shrunk)
    lane = lax.broadcasted_iota(jnp.int32, (tokens, HEAD_WIDTH), 1)
    per = HEAD_WIDTH // RANK
    spread = []
    for c in range(page_axis // per):
        group = c * per + lane // RANK
        adapter = (group % NX) * nz + group // NX
        spread.append(jnp.where(adapter_col[...] == adapter, shrunk, 0.0).astype(jnp.bfloat16))
    spread = jnp.concatenate(spread, axis=1)
    delta = jnp.dot(
        spread,
        ga[:, :, 0:RANK, :].reshape(page_axis * RANK, cols),
        preferred_element_type=jnp.float32,
    )
    acc[...] += delta

    token = me * tokens + lax.broadcasted_iota(jnp.int32, (tokens, HEAD_WIDTH), 0)
    angle = (token - start_col[...]).astype(jnp.float32) * freq_ref[...]
    cosine[...] = jnp.cos(angle)
    sine[...] = jnp.where(lane < HEAD_WIDTH // 2, -jnp.sin(angle), jnp.sin(angle))
    for h in range(heads):
        u = acc[:, h * HEAD_WIDTH : (h + 1) * HEAD_WIDTH]
        turned = u * cosine[...] + pltpu.roll(u, HEAD_WIDTH // 2, 1) * sine[...]
        query_ref[:, h * HEAD_WIDTH : (h + 1) * HEAD_WIDTH] = turned.astype(jnp.bfloat16)

    lax.fori_loop(early + nz // 2 + 1, nz + 1, late_step, 0)

    factor = math.log2(math.e) / math.sqrt(HEAD_WIDTH)
    lane = lax.broadcasted_iota(jnp.int32, (tokens, HEAD_WIDTH), 1)
    begin = start_col[...] - lane
    row = lax.broadcasted_iota(jnp.int32, (tokens, HEAD_WIDTH), 0)
    pieces = tokens // HEAD_WIDTH

    def attend(h, carry):
        where_h = pl.ds(pl.multiple_of(h * HEAD_WIDTH, HEAD_WIDTH), HEAD_WIDTH)
        query = query_ref[:, where_h]

        def score(offset, top, causal):
            block = lax.dot_general(
                query,
                kvb[offset, 0],
                (((1,), (1,)), ((), ())),
                preferred_element_type=jnp.float32,
            )
            base = (me - offset) * tokens
            for c in range(pieces):
                visible = begin <= base + c * HEAD_WIDTH
                if causal:
                    visible = visible & (lane + c * HEAD_WIDTH <= row)
                part = block[:, c * HEAD_WIDTH : (c + 1) * HEAD_WIDTH]
                part = jnp.where(visible, part, MASKED)
                scores[offset, :, c * HEAD_WIDTH : (c + 1) * HEAD_WIDTH] = part
                top = part if top is None else jnp.maximum(top, part)
            return top

        top = score(0, None, True)
        top = lax.fori_loop(1, nz + 1, lambda o, t: score(o, t, False), top)
        top = jnp.broadcast_to(jnp.max(top, axis=1, keepdims=True), (tokens, HEAD_WIDTH))
        ones = jnp.ones((tokens, HEAD_WIDTH), jnp.bfloat16)

        def mix(offset, total):
            weight = []
            for c in range(pieces):
                part = scores[offset, :, c * HEAD_WIDTH : (c + 1) * HEAD_WIDTH]
                weight.append(jnp.exp2((part - top) * factor).astype(jnp.bfloat16))
            weight = jnp.concatenate(weight, axis=1)
            value = jnp.concatenate([kvb[offset, 1], ones], axis=1)
            return total + jnp.dot(weight, value, preferred_element_type=jnp.float32)

        total = lax.fori_loop(
            0, nz + 1, mix, jnp.zeros((tokens, 2 * HEAD_WIDTH), jnp.float32)
        )
        out_ref[:, where_h] = (total[:, :HEAD_WIDTH] / total[:, HEAD_WIDTH:]).astype(
            jnp.bfloat16
        )
        return carry

    lax.fori_loop(0, heads, attend, 0)

    def finish(i, carry):
        a_finish(i)
        w_finish(i)
        return carry

    lax.fori_loop(0, nz, finish, 0)
    for step in range(1, nh):
        head_copy(step).wait_send()

    def kv_finish(j, carry):
        reach_up = reach(j)
        for half in range(2):

            @pl.when(j + 1 <= reach_up)
            def _():
                kv_forward(j, half).wait_send()

            @pl.when((j > 0) & (j > reach_up) & (j - 1 > reach_up))
            def _():
                kv_backward(j, half).wait_send()

        return carry

    lax.fori_loop(0, nz + 1, kv_finish, 0)
    for half in range(2):
        kv_cross(half).wait_send()


def body(
    nz,
    nh,
    hidden,
    attention_norm_gain,
    wq,
    adapter_down_weight,
    adapter_up_weight,
    key_value_cache,
    logical_page_table,
    lengths,
    prompt_adapter_index,
):
    tokens, width = hidden.shape
    feat, cols = wq.shape
    own_width = adapter_down_weight.shape[0]
    pages = logical_page_table.shape[1]
    kv = key_value_cache.reshape(pages, tokens // pages, 2 * HEAD_WIDTH)
    half = HEAD_WIDTH // 2
    freq = ROPE_BASE ** (-(jnp.arange(half, dtype=jnp.float32) * 2.0 / HEAD_WIDTH))
    freq = jnp.concatenate([freq, freq])[None, :]
    smem = pl.BlockSpec(memory_space=pltpu.SMEM)
    vmem = pl.BlockSpec(memory_space=pltpu.VMEM)
    dma = pltpu.SemaphoreType.DMA
    bf16, f32, i32 = jnp.bfloat16, jnp.float32, jnp.int32
    return pl.pallas_call(
        functools.partial(kernel, nz, nh),
        name="project_attend",
        out_shape=(
            jax.ShapeDtypeStruct((tokens, cols), bf16),
            jax.ShapeDtypeStruct((tokens, cols), bf16),
        ),
        in_specs=[smem] * 3 + [vmem] * 7,
        out_specs=(vmem, vmem),
        scratch_shapes=[
            pltpu.VMEM((nz, tokens, NX * feat), bf16),
            pltpu.VMEM((tokens, own_width), bf16),
            pltpu.VMEM((nz, NX, 2 * RANK, cols), bf16),
            pltpu.VMEM((nz, NX, feat, cols), bf16),
            pltpu.VMEM((nz + 1, 2, tokens, HEAD_WIDTH), bf16),
            pltpu.VMEM((tokens, cols), f32),
            pltpu.VMEM((tokens, HEAD_WIDTH), i32),
            pltpu.VMEM((tokens, HEAD_WIDTH), i32),
            pltpu.VMEM((8, tokens), i32),
            pltpu.VMEM((tokens, HEAD_WIDTH), f32),
            pltpu.VMEM((tokens, HEAD_WIDTH), f32),
            pltpu.VMEM((RANK, tokens), f32),
            pltpu.VMEM((nh, RANK, tokens), f32),
            pltpu.VMEM((nz + 1, tokens, tokens), f32),
            dma((nz, NX)),
            dma((nz, NX)),
            dma((nz + 1,)),
            dma((nz + 1,)),
            dma((3, nz)),
            dma((3, nz)),
            dma((nz + 1, 2)),
            dma((nz + 1, 2)),
            dma((nz + 1, 2)),
            dma((nh,)),
            dma((nh,)),
        ],
        compiler_params=pltpu.CompilerParams(
            collective_id=0, has_side_effects=True, vmem_limit_bytes=58 << 20
        ),
    )(
        lengths,
        prompt_adapter_index,
        logical_page_table,
        hidden,
        attention_norm_gain[None, :],
        wq,
        adapter_down_weight,
        adapter_up_weight,
        kv,
        freq,
    )


def solution(mesh):
    return jax.shard_map(
        functools.partial(body, mesh.shape["page"] // NX, mesh.shape["head"]),
        mesh=mesh,
        in_specs=(
            P("page", None),
            P(),
            P("page", "head"),
            P("head", "page"),
            P("page", "head"),
            P("page", None, "head"),
            P("page", None),
            P(),
            P(),
        ),
        out_specs=(P("page", "head"), P("page", "head")),
        check_vma=False,
    )
```

time: 496 us -> 159 us (0.32)
  waiting for transfers between devices: 277 us -> 0 us
  Pallas kernels: 0 us -> 150 us
  starting transfers between devices: 85.5 us -> 0 us
  matrix products: 43.5 us -> 0 us
  other arithmetic: 32.2 us -> 0.62 us
  blocking collectives: 20 us -> 0 us
  local copies, waits for them, and re-layouts: 22.2 us -> 8.04 us
  between operations: 14 us -> 0.64 us
    all_gather x3 -> x0, waiting for transfers between devices: 217 us -> none  [the longest x1 131 us: body(): lax.all_gather(adapter_up_weight, 'page', axis=0, tiled=True)]
    pallas_call x0 -> x1, Pallas kernels: none -> 150 us  [body(): pl.pallas_call(functools.partial(kernel, nz, nh), name='project_attend',...]
    ppermute x16 -> x0, starting transfers between devices: 85.4 us -> none  [from_behind(): lax.ppermute(value, axis, [(source, source + steps) for source in range(l...]
    ppermute x16 -> x0, waiting for transfers between devices: 57.9 us -> none  [from_behind(): lax.ppermute(value, axis, [(source, source + steps) for source in range(l...]
    dot_general x11 -> x0, matrix products: 43.5 us -> none  [the longest x4 16.8 us: score_block(): lax.dot_general(query, keyblock, (((1,), (1,)), ((), ())), preferred_elem...]
    psum x1 -> x0, blocking collectives: 20 us -> none  [body(): shrunk = lax.psum(partial_sum, 'head').astype(jnp.bfloat16)]
    reduce_sum x7 -> x0, other arithmetic: 17.4 us -> none  [the longest x4 13.9 us: normalize(): return (expo / jnp.sum(expo, axis=-1, keepdims=True)).astype(jnp.bfloat16)]
    dynamic_update_slice x16 -> x0, local copies, waits for them, and re-layouts: 11.2 us -> none  [body(): unused_last, earlier = lax.scan(pass_on, own_block, None, length=span_count)]
  transfers between devices with their start and end apart: 19 -> 0, of which waited for: 18 -> 0; matrix products, arithmetic and copies ran while one was open for 9% -> 0% of each run, Pallas kernels for 0% -> 0%
where the time goes in v1:
time: 159 us
  Pallas kernels  150 us (94%)
  local copies, waits for them, and re-layouts  8.04 us (5%)
    pallas_call x1, Pallas kernels, body(): pl.pallas_call(functools.partial(kernel, nz, nh), name='project_attend',...  150 us
    unnamed x3, local copies, waits for them, and re-layouts  5.01 us

profile of v1, /device:TPU:24, one launch (start us, length us, event | category | flops | bytes accessed | tf_op | source)
XLA Modules:
  0.0 159.0 jit_solution(9773466799493154712)
XLA Ops:
  0.6 0.6 maximum_bitcast_fusion.freq_ref
  1.3 1.3 broadcast_in_dim.6.gain_ref
  2.6 1.5 copy.11.down_ref
  4.0 1.7 %reshape.7.kv_ref = bf16[3,128,256]{2,1,0:T(8,128)(2,1)} reshape(bf16[384,2,128]{2,1,0:T(2,128)(2,1)} %param.14) | data formatting | bytes 393216 | tf_op jit(solution)/shard_map/reshape | solution.py:519
  5.8 149.7 %project_attend.1 = (bf16[384,512]{1,0:T(8,128)(2,1)}, bf16[384,512]{1,0:T(8,128)(2,1)}) custom-call(s32[16]{0:T(128)} %length_ref.1, s32[16]{0:T(128)} %prompt_adapter_ref.1, s32[1,3]{1,0:T(1,128)} %table_ref.1, bf16[384,4096]{1,0:T(8,128)(2,1)} %hidden_ref.1, bf16[1,4096]{1,0:T(2,128)(2,1)} %broadcast_in_dim.6.gain_ref, bf16[64,512]{1,0:T(8,128)(2,1)} %wq_ref.1, ...), custom_call_target="tpu_custom_call" | custom-call | tf_op jit(solution)/shard_map/project_attend/pallas_call | solution.py:527
  155.5 1.8 %copy.14 = bf16[384,512]{1,0:T(8,128)(2,1)} copy(bf16[384,512]{1,0:T(8,128)(2,1)} %get-tuple-element.4) | data formatting | bytes 786432
  157.3 1.8 %copy.15 = bf16[384,512]{1,0:T(8,128)(2,1)} copy(bf16[384,512]{1,0:T(8,128)(2,1)} %get-tuple-element.5) | data formatting | bytes 786432
  (1 shorter events, 0.0 us)

commit v2 on v1

v2 whole, which is shorter than its diff:
```python
import functools
import math

import jax
import jax.numpy as jnp
import numpy as np
from jax import lax
from jax.experimental import pallas as pl
from jax.experimental.pallas import tpu as pltpu
from jax.sharding import PartitionSpec as P

HEAD_WIDTH = 128
RANK = 16
EPSILON = 1e-05
ROPE_BASE = 500000.0
NX = 4
MASKED = -1e30
LAG_NEAR = 2
LAG_FAR = 4
UNROLL = 4


def clamp(value, low, high):
    return jnp.minimum(jnp.maximum(value, low), high)


def kernel(
    nz,
    nh,
    length_ref,
    prompt_adapter_ref,
    table_ref,
    hidden_any,
    gain_ref,
    wq_ref,
    down_ref,
    up_ref,
    kv_ref,
    freq_ref,
    query_ref,
    out_ref,
    hidden_ref,
    gain,
    normed,
    own_feat,
    ga,
    share,
    share_in,
    slots,
    gw,
    kvb,
    acc,
    start_col,
    slot_col,
    slot_row,
    cosine,
    sine,
    psum,
    scores,
    tops,
    hidden_sem,
    recv_a,
    send_a,
    recv_w,
    send_zw,
    send_xw,
    recv_rs,
    send_rs,
    recv_ag,
    send_ag,
    recv_kv,
    send_kf,
    send_kb,
    recv_h,
    send_h,
):
    page_axis = NX * nz
    tokens, width = hidden_ref.shape
    feat = wq_ref.shape[0]
    cols = wq_ref.shape[1]
    heads = cols // HEAD_WIDTH
    own_width = own_feat.shape[1]
    requests = length_ref.shape[0]
    quarter = requests // NX
    pages = kv_ref.shape[0]
    page_rows = kv_ref.shape[1]
    me = lax.axis_index("page")
    head = lax.axis_index("head")
    x = me // nz
    z = me % nz
    z_up = x * nz + (z + 1) % nz
    z_down = x * nz + (z + nz - 1) % nz
    p_up = (me + 1) % page_axis
    p_down = (me + page_axis - 1) % page_axis
    left_x = (x + NX - 1) % NX
    right_x = (x + 1) % NX
    far_x = (x + 2) % NX
    x_up = right_x * nz + z
    x_down = left_x * nz + z
    x_far = far_x * nz + z

    hidden_copy = pltpu.make_async_copy(hidden_any, hidden_ref, hidden_sem)
    hidden_copy.start()

    def send(src, dst, send_sem, recv_sem, page):
        return pltpu.make_async_remote_copy(
            src_ref=src,
            dst_ref=dst,
            send_sem=send_sem,
            recv_sem=recv_sem,
            device_id={"page": page},
            device_id_type=pl.DeviceIdType.MESH,
        )

    barrier = pltpu.get_barrier_semaphore()
    greeted = (z_up, z_down, x_up, x_down, x_far, p_up, p_down)
    for page in greeted:
        pl.semaphore_signal(
            barrier, inc=1, device_id={"page": page}, device_id_type=pl.DeviceIdType.MESH
        )
    for step in range(1, nh):
        pl.semaphore_signal(
            barrier,
            inc=1,
            device_id={"head": (head + step) % nh},
            device_id_type=pl.DeviceIdType.MESH,
        )

    ga[z, 0:RANK, :] = up_ref[...]
    ga[z, RANK : 2 * RANK, :] = down_ref[...]
    gw[z, x] = wq_ref[...]
    for j in range(pages):
        page_block = kv_ref[table_ref[0, j]]
        kvb[0, 0, j * page_rows : (j + 1) * page_rows, :] = page_block[:, :HEAD_WIDTH]
        kvb[0, 1, j * page_rows : (j + 1) * page_rows, :] = page_block[:, HEAD_WIDTH:]
    pl.semaphore_wait(barrier, len(greeted) + nh - 1)

    low = nz * 5 // 16
    high = nz - 1 - low

    def reach(offset):
        return clamp(nz - 1 - (z + 2 * nz - offset) % nz, low, high)

    def kv_forward(offset, half):
        return send(
            kvb.at[offset, half],
            kvb.at[offset + 1, half],
            send_kf.at[offset, half],
            recv_kv.at[offset + 1, half],
            p_up,
        )

    def kv_backward(offset, half):
        return send(
            kvb.at[offset, half],
            kvb.at[offset - 1, half],
            send_kb.at[offset, half],
            recv_kv.at[offset - 1, half],
            p_down,
        )

    def kv_cross(half):
        return send(
            kvb.at[0, half],
            kvb.at[nz, half],
            send_kb.at[0, half],
            recv_kv.at[nz, half],
            x_up,
        )

    def kv_wait(offset, half):
        send(
            kvb.at[0, half],
            kvb.at[offset, half],
            send_kb.at[0, half],
            recv_kv.at[offset, half],
            x_up,
        ).wait_recv()

    def kv_step(j):
        reach_up = reach(j)
        back = nz + 1 - j
        reach_back = reach(back)
        for half in range(2):

            @pl.when(j <= reach_up)
            def _():
                kv_wait(j, half)

                @pl.when(j + 1 <= reach_up)
                def _():
                    kv_forward(j, half).start()

            @pl.when(back > reach_back)
            def _():
                kv_wait(back, half)

                @pl.when(back - 1 > reach_back)
                def _():
                    kv_backward(back, half).start()

    def position(i):
        distance = (i + 1) // 2
        return jnp.where(i % 2 == 1, (z + nz - distance) % nz, (z + distance) % nz)

    def goes_up(i):
        return ((i % 2 == 1) & ((i + 1) // 2 < nz // 2)) | (i == 0)

    def goes_down(i):
        return (i % 2 == 0) & ((i + 1) // 2 < nz // 2 - 1)

    def down_slot(i):
        return jnp.where(i == 0, nz, i)

    def a_copy(i, page, slot):
        zz = position(i)
        return send(ga.at[zz], ga.at[zz], send_a.at[slot], recv_a.at[zz], page)

    def w_copy(i, page, slot):
        zz = position(i)
        return send(gw.at[zz, x], gw.at[zz, x], send_zw.at[slot], recv_w.at[zz, x], page)

    def forward_z(i):
        @pl.when(goes_up(i))
        def _():
            a_copy(i, z_up, i).start()
            w_copy(i, z_up, i).start()

        @pl.when(goes_down(i))
        def _():
            a_copy(i, z_down, down_slot(i)).start()
            w_copy(i, z_down, down_slot(i)).start()

    def arrive_z(i):
        for copy in (a_copy, w_copy):
            copy(i, z_up, i).wait_recv()

            @pl.when(goes_up(i))
            def _():
                copy(i, z_up, i).start()

            @pl.when(goes_down(i))
            def _():
                copy(i, z_down, down_slot(i)).start()

    def x_copy(i, xx, page, which):
        zz = position(i)
        return send(
            gw.at[zz, xx], gw.at[zz, xx], send_xw.at[which, zz], recv_w.at[zz, xx], page
        )

    def spread_x(i):
        x_copy(i, x, x_up, 0).start()
        x_copy(i, x, x_down, 1).start()

    def near(i):
        x_copy(i, left_x, x_up, 2).wait_recv()

        @pl.when(i % 2 == 0)
        def _():
            x_copy(i, left_x, x_up, 2).start()

        x_copy(i, right_x, x_down, 2).wait_recv()

        @pl.when(i % 2 == 1)
        def _():
            x_copy(i, right_x, x_down, 2).start()

    peers = ((right_x, x_up), (left_x, x_down), (far_x, x_far))

    def share_copy(k):
        xx, page = peers[k]
        return send(
            share.at[pl.ds(xx * quarter, quarter)],
            share_in.at[k],
            send_rs.at[k],
            recv_rs.at[k],
            page,
        )

    def slot_copy(k):
        mine = pl.ds(x * quarter, quarter)
        return send(slots.at[mine], slots.at[mine], send_ag.at[k], recv_ag.at[x], peers[k][1])

    def make_share():
        for r in range(requests):
            wanted = prompt_adapter_ref[r] - x * nz
            block = ga[jnp.minimum(jnp.maximum(wanted, 0), nz - 1)].astype(jnp.float32)
            held = jnp.where((wanted >= 0) & (wanted < nz), 1.0, 0.0)
            share[r] = (block * held).astype(jnp.bfloat16)
        for k in range(3):
            share_copy(k).start()

    def sum_share():
        for k in range(3):
            share_copy(k).wait_recv()
        mine = pl.ds(x * quarter, quarter)
        total = share[mine].astype(jnp.float32)
        for k in range(3):
            total = total + share_in[k].astype(jnp.float32)
        slots[mine] = total.astype(jnp.bfloat16)
        for k in range(3):
            slot_copy(k).start()

    def head_copy(step):
        return pltpu.make_async_remote_copy(
            src_ref=psum.at[0],
            dst_ref=psum.at[step],
            send_sem=send_h.at[step],
            recv_sem=recv_h.at[step],
            device_id={"head": (head + step) % nh},
            device_id_type=pl.DeviceIdType.MESH,
        )

    def use_slots():
        for xx in (left_x, right_x, far_x):
            theirs = pl.ds(xx * quarter, quarter)
            send(
                slots.at[theirs], slots.at[theirs], send_ag.at[0], recv_ag.at[xx], x_up
            ).wait_recv()
        part = lax.dot_general(
            slots[:, RANK : 2 * RANK, :].reshape(requests * RANK, cols),
            own_feat[...],
            (((1,), (1,)), ((), ())),
            preferred_element_type=jnp.float32,
        )
        wanted = slot_row[...]
        wanted = jnp.concatenate([wanted, wanted], axis=0)
        total = jnp.zeros((RANK, tokens), jnp.float32)
        for r in range(requests):
            total += jnp.where(wanted == r, part[r * RANK : (r + 1) * RANK], 0.0)
        psum[0] = total
        for step in range(1, nh):
            head_copy(step).start()

    forward_z(0)
    spread_x(0)
    for half in range(2):

        @pl.when(reach(0) >= 1)
        def _():
            kv_forward(0, half).start()

        kv_cross(half).start()

    def prompts(token):
        start = jnp.zeros(token.shape, jnp.int32)
        slot = jnp.zeros(token.shape, jnp.int32)
        end = jnp.int32(0)
        for r in range(requests):
            begin = end
            end = end + length_ref[r]
            inside = token >= begin
            start = jnp.where(inside, begin, start)
            slot = jnp.where(inside, r, slot)
        return start, slot

    slot_row[...] = prompts(
        me * tokens + lax.broadcasted_iota(jnp.int32, (8, tokens), 1)
    )[1]
    gain[...] = gain_ref[...].astype(jnp.float32)
    acc[...] = jnp.zeros_like(acc)
    hidden_copy.wait()

    rows_step = 32
    norm_steps = tokens // rows_step
    norm_each = (norm_steps + LAG_FAR - 1) // LAG_FAR

    def norm_rows(step, carry):
        rows = pl.ds(pl.multiple_of(step * rows_step, rows_step), rows_step)
        value = hidden_ref[rows, :].astype(jnp.float32)
        scale = lax.rsqrt(jnp.mean(value * value, axis=-1, keepdims=True) + EPSILON)
        lane = lax.broadcasted_iota(jnp.int32, (rows_step, 2 * feat), 1)
        lower = lane < feat
        for pair in range(nz // 2):
            piece = []
            for k in range(NX):
                c = k * nz // 2 + pair
                part = value[:, c * 2 * feat : (c + 1) * 2 * feat] * scale
                piece.append(part * gain[c : c + 1, :])
            for k in range(0, NX, 2):
                even = jnp.where(lower, piece[k], pltpu.roll(piece[k + 1], feat, 1))
                odd = jnp.where(lower, pltpu.roll(piece[k], feat, 1), piece[k + 1])
                normed[2 * pair, rows, k * feat : (k + 2) * feat] = even.astype(jnp.bfloat16)
                normed[2 * pair + 1, rows, k * feat : (k + 2) * feat] = odd.astype(jnp.bfloat16)
        for k in range(own_width // HEAD_WIDTH):
            c = head * (own_width // HEAD_WIDTH) + k
            lanes = pl.ds(pl.multiple_of(c * HEAD_WIDTH, HEAD_WIDTH), HEAD_WIDTH)
            own = hidden_ref[rows, lanes].astype(jnp.float32) * scale * gain[pl.ds(c, 1), :]
            own_feat[rows, k * HEAD_WIDTH : (k + 1) * HEAD_WIDTH] = own.astype(jnp.bfloat16)
        token = me * tokens + step * rows_step + lax.broadcasted_iota(
            jnp.int32, (rows_step, HEAD_WIDTH), 0
        )
        start, slot = prompts(token)
        start_col[rows, :] = start
        slot_col[rows, :] = slot
        return carry

    lane = lax.broadcasted_iota(jnp.int32, (tokens, HEAD_WIDTH), 1)

    def rotation():
        token = me * tokens + lax.broadcasted_iota(jnp.int32, (tokens, HEAD_WIDTH), 0)
        angle = (token - start_col[...]).astype(jnp.float32) * freq_ref[...]
        cosine[...] = jnp.cos(angle)
        turn = jnp.sin(angle)
        sine[...] = jnp.where(lane < HEAD_WIDTH // 2, -turn, turn)

    def at(m, when, body):
        @pl.when(m == when)
        def _():
            body()

    last_z = 3 * (nz // 4) - 1 if nz % 4 == 0 else nz // 2
    kv_early = nz // 5

    def weights_step(m, carry):
        distance = 2 * (m // 3) + m % 3

        @pl.when((m % 3 != 0) & (distance <= nz // 2))
        def _():
            arrive_z(2 * distance - 1)

            @pl.when(distance < nz // 2)
            def _():
                arrive_z(2 * distance)

        @pl.when((m >= 1) & (m < nz))
        def _():
            spread_x(m)

        @pl.when((m >= LAG_NEAR) & (m < nz + LAG_NEAR))
        def _():
            near(m - LAG_NEAR)

        @pl.when(m < LAG_FAR)
        def _():
            lax.fori_loop(
                m * norm_each,
                jnp.minimum((m + 1) * norm_each, norm_steps),
                norm_rows,
                0,
            )

        at(m, LAG_FAR + 1, rotation)
        at(m, last_z, make_share)
        at(m, last_z + 2, sum_share)
        at(m, last_z + 4, use_slots)

        @pl.when((m % 3 == 0) & (m >= 3) & (m // 3 <= kv_early))
        def _():
            kv_step(m // 3)

        late = m - 3 * kv_early
        @pl.when((late > 0) & (late % 2 == 1) & (kv_early + (late + 1) // 2 <= nz))
        def _():
            kv_step(kv_early + (late + 1) // 2)

        @pl.when(m >= LAG_FAR)
        def _():
            i = m - LAG_FAR
            zz = position(i)
            x_copy(i, far_x, x_up, 2).wait_recv()
            acc[...] += jnp.dot(
                normed[zz], gw[zz].reshape(NX * feat, cols), preferred_element_type=jnp.float32
            )

        return carry

    count = max(nz + LAG_FAR, last_z + 5)
    assert count == nz + LAG_FAR or nz < 16
    lax.fori_loop(0, nz + LAG_FAR, weights_step, 0)
    if last_z + 4 >= nz + LAG_FAR:
        use_slots()
    kv_next = kv_early + (nz + LAG_FAR - 1 - 3 * kv_early + 1) // 2 + 1

    def service(limit):
        nonlocal kv_next
        while kv_next <= min(limit, nz):
            kv_step(jnp.int32(kv_next))
            kv_next += 1

    first_late = kv_next
    service(first_late)

    for step in range(1, nh):
        head_copy(step).wait_recv()
    shrunk = psum[0]
    for step in range(1, nh):
        shrunk = shrunk + psum[step]
    shrunk = shrunk.astype(jnp.bfloat16).astype(jnp.float32)
    shrunk = jnp.concatenate([shrunk] * (HEAD_WIDTH // RANK), axis=0)
    shrunk = jnp.transpose(shrunk)
    per = HEAD_WIDTH // RANK
    spread = []
    for c in range(requests // per):
        wanted = c * per + lane // RANK
        spread.append(jnp.where(slot_col[...] == wanted, shrunk, 0.0).astype(jnp.bfloat16))
    spread = jnp.concatenate(spread, axis=1)
    acc[...] += jnp.dot(
        spread,
        slots[:, 0:RANK, :].reshape(requests * RANK, cols),
        preferred_element_type=jnp.float32,
    )

    for h in range(heads):
        u = acc[:, h * HEAD_WIDTH : (h + 1) * HEAD_WIDTH]
        turned = u * cosine[...] + pltpu.roll(u, HEAD_WIDTH // 2, 1) * sine[...]
        query_ref[:, h * HEAD_WIDTH : (h + 1) * HEAD_WIDTH] = turned.astype(jnp.bfloat16)

    service(first_late + 1)

    factor = math.log2(math.e) / math.sqrt(HEAD_WIDTH)
    begin = start_col[...] - lane
    row = lax.broadcasted_iota(jnp.int32, (tokens, HEAD_WIDTH), 0)
    pieces = tokens // HEAD_WIDTH
    ones = jnp.ones((tokens, HEAD_WIDTH), jnp.bfloat16)

    def lanes_of(h):
        return pl.ds(pl.multiple_of(h * HEAD_WIDTH, HEAD_WIDTH), HEAD_WIDTH)

    def score(h, buffer, offset, top, causal):
        block = lax.dot_general(
            query_ref[:, lanes_of(h)],
            kvb[offset, 0],
            (((1,), (1,)), ((), ())),
            preferred_element_type=jnp.float32,
        )
        base = (me - offset) * tokens
        for c in range(pieces):
            visible = begin <= base + c * HEAD_WIDTH
            if causal:
                visible = visible & (lane + c * HEAD_WIDTH <= row)
            part = block[:, c * HEAD_WIDTH : (c + 1) * HEAD_WIDTH]
            part = jnp.where(visible, part, MASKED)
            scores[buffer, offset, :, c * HEAD_WIDTH : (c + 1) * HEAD_WIDTH] = part
            top = part if top is None else jnp.maximum(top, part)
        return top

    def score_early(h, buffer):
        top = score(h, buffer, 0, None, True)

        def one(k, top):
            offset = jnp.where(k < low, k + 1, nz - 2 * low + 1 + k)
            return score(h, buffer, offset, top, False)

        tops[buffer] = lax.fori_loop(0, 2 * low, one, top, unroll=UNROLL)

    def score_late(h, buffer):
        return lax.fori_loop(
            low + 1,
            nz - low + 1,
            lambda o, t: score(h, buffer, o, t, False),
            tops[buffer],
            unroll=UNROLL,
        )

    def finish_head(h, buffer, top):
        top = jnp.broadcast_to(jnp.max(top, axis=1, keepdims=True), (tokens, HEAD_WIDTH))

        def mix(offset, total):
            weight = []
            for c in range(pieces):
                part = scores[buffer, offset, :, c * HEAD_WIDTH : (c + 1) * HEAD_WIDTH]
                weight.append(jnp.exp2((part - top) * factor).astype(jnp.bfloat16))
            weight = jnp.concatenate(weight, axis=1)
            value = jnp.concatenate([kvb[offset, 1], ones], axis=1)
            return total + jnp.dot(weight, value, preferred_element_type=jnp.float32)

        total = lax.fori_loop(
            0,
            nz + 1,
            mix,
            jnp.zeros((tokens, 2 * HEAD_WIDTH), jnp.float32),
            unroll=UNROLL,
        )
        out_ref[:, lanes_of(h)] = (total[:, :HEAD_WIDTH] / total[:, HEAD_WIDTH:]).astype(
            jnp.bfloat16
        )

    score_early(0, 0)
    service(first_late + 2)
    score_early(1, 1)
    service(nz)

    def attend(h, carry):
        buffer = h % 2

        @pl.when(h >= 2)
        def _():
            score_early(h, buffer)

        finish_head(h, buffer, score_late(h, buffer))
        return carry

    lax.fori_loop(0, heads, attend, 0)

    def finish(i, carry):
        @pl.when(goes_up(i))
        def _():
            a_copy(i, z_up, i).wait_send()
            w_copy(i, z_up, i).wait_send()

        @pl.when(goes_down(i))
        def _():
            a_copy(i, z_down, down_slot(i)).wait_send()
            w_copy(i, z_down, down_slot(i)).wait_send()

        x_copy(i, x, x_up, 0).wait_send()
        x_copy(i, x, x_down, 1).wait_send()
        x_copy(i, left_x, x_up, 2).wait_send()
        return carry

    lax.fori_loop(0, nz, finish, 0)
    for k in range(3):
        share_copy(k).wait_send()
        slot_copy(k).wait_send()
    for step in range(1, nh):
        head_copy(step).wait_send()

    def kv_finish(j, carry):
        reach_up = reach(j)
        for half in range(2):

            @pl.when(j + 1 <= reach_up)
            def _():
                kv_forward(j, half).wait_send()

            @pl.when(j - 1 > reach_up)
            def _():
                kv_backward(j, half).wait_send()

        return carry

    lax.fori_loop(0, nz + 1, kv_finish, 0)
    for half in range(2):
        kv_cross(half).wait_send()


def body(
    nz,
    nh,
    hidden,
    attention_norm_gain,
    wq,
    adapter_down_weight,
    adapter_up_weight,
    key_value_cache,
    logical_page_table,
    lengths,
    prompt_adapter_index,
):
    tokens, width = hidden.shape
    feat, cols = wq.shape
    own_width = adapter_down_weight.shape[0]
    pages = logical_page_table.shape[1]
    requests = lengths.shape[0]
    kv = key_value_cache.reshape(pages, tokens // pages, 2 * HEAD_WIDTH)
    half = HEAD_WIDTH // 2
    freq = ROPE_BASE ** (-(np.arange(half, dtype=np.float64) * 2.0 / HEAD_WIDTH))
    freq = np.concatenate([freq, freq])[None, :].astype(np.float32)
    smem = pl.BlockSpec(memory_space=pltpu.SMEM)
    vmem = pl.BlockSpec(memory_space=pltpu.VMEM)
    dma = pltpu.SemaphoreType.DMA
    bf16, f32, i32 = jnp.bfloat16, jnp.float32, jnp.int32
    return pl.pallas_call(
        functools.partial(kernel, nz, nh),
        name="project_attend",
        out_shape=(
            jax.ShapeDtypeStruct((tokens, cols), bf16),
            jax.ShapeDtypeStruct((tokens, cols), bf16),
        ),
        in_specs=[smem] * 3 + [pl.BlockSpec(memory_space=pl.ANY)] + [vmem] * 6,
        out_specs=(vmem, vmem),
        scratch_shapes=[
            pltpu.VMEM((tokens, width), bf16),
            pltpu.VMEM((width // HEAD_WIDTH, HEAD_WIDTH), f32),
            pltpu.VMEM((nz, tokens, NX * feat), bf16),
            pltpu.VMEM((tokens, own_width), bf16),
            pltpu.VMEM((nz, 2 * RANK, cols), bf16),
            pltpu.VMEM((requests, 2 * RANK, cols), bf16),
            pltpu.VMEM((3, requests // NX, 2 * RANK, cols), bf16),
            pltpu.VMEM((requests, 2 * RANK, cols), bf16),
            pltpu.VMEM((nz, NX, feat, cols), bf16),
            pltpu.VMEM((nz + 1, 2, tokens, HEAD_WIDTH), bf16),
            pltpu.VMEM((tokens, cols), f32),
            pltpu.VMEM((tokens, HEAD_WIDTH), i32),
            pltpu.VMEM((tokens, HEAD_WIDTH), i32),
            pltpu.VMEM((8, tokens), i32),
            pltpu.VMEM((tokens, HEAD_WIDTH), f32),
            pltpu.VMEM((tokens, HEAD_WIDTH), f32),
            pltpu.VMEM((nh, RANK, tokens), f32),
            pltpu.VMEM((2, nz + 1, tokens, tokens), f32),
            pltpu.VMEM((2, tokens, HEAD_WIDTH), f32),
            dma(()),
            dma((nz,)),
            dma((nz + 1,)),
            dma((nz, NX)),
            dma((nz + 1,)),
            dma((3, nz)),
            dma((3,)),
            dma((3,)),
            dma((NX,)),
            dma((3,)),
            dma((nz + 1, 2)),
            dma((nz + 1, 2)),
            dma((nz + 1, 2)),
            dma((nh,)),
            dma((nh,)),
        ],
        compiler_params=pltpu.CompilerParams(
            collective_id=0, has_side_effects=True, vmem_limit_bytes=58 << 20
        ),
    )(
        lengths,
        prompt_adapter_index,
        logical_page_table,
        hidden,
        attention_norm_gain.reshape(width // HEAD_WIDTH, HEAD_WIDTH),
        wq,
        adapter_down_weight.T,
        adapter_up_weight,
        kv,
        freq,
    )


def solution(mesh):
    return jax.shard_map(
        functools.partial(body, mesh.shape["page"] // NX, mesh.shape["head"]),
        mesh=mesh,
        in_specs=(
            P("page", None),
            P(),
            P("page", "head"),
            P("head", "page"),
            P("page", "head"),
            P("page", None, "head"),
            P("page", None),
            P(),
            P(),
        ),
        out_specs=(P("page", "head"), P("page", "head")),
        check_vma=False,
    )
```

time: 159 us -> 124 us (0.78); the launches traced: 159 us -> 122 us
  Pallas kernels: 150 us -> 116 us
  local copies, waits for them, and re-layouts: 8.04 us -> 5.26 us
    pallas_call x1, Pallas kernels: 150 us -> 116 us  [body(): pl.pallas_call(functools.partial(kernel, nz, nh), name='project_attend',...]
    unnamed x3 -> x2, local copies, waits for them, and re-layouts: 5.01 us -> 3.53 us
where the time goes in v2:
time: 124 us; the launch traced here: 122 us
  Pallas kernels  116 us (94%)
  local copies, waits for them, and re-layouts  5.26 us (4%)
    pallas_call x1, Pallas kernels, body(): pl.pallas_call(functools.partial(kernel, nz, nh), name='project_attend',...  116 us
    unnamed x2, local copies, waits for them, and re-layouts  3.53 us

profile of v2, /device:TPU:24, one launch (start us, length us, event | category | flops | bytes accessed | tf_op | source)
XLA Modules:
  0.0 122.2 jit_solution(10975365537114046339)
XLA Ops:
  0.6 1.7 %reshape.11.kv_ref = bf16[3,128,256]{2,1,0:T(8,128)(2,1)} reshape(bf16[384,2,128]{2,1,0:T(2,128)(2,1)} %param.15) | data formatting | bytes 393216 | tf_op jit(solution)/shard_map/reshape | solution.py:657
  2.4 116.3 %project_attend.1 = (bf16[384,512]{1,0:T(8,128)(2,1)}, bf16[384,512]{1,0:T(8,128)(2,1)}) custom-call(s32[16]{0:T(128)} %length_ref.1, s32[16]{0:T(128)} %prompt_adapter_ref.1, s32[1,3]{1,0:T(1,128)} %table_ref.1, bf16[384,4096]{1,0:T(8,128)(2,1)} %hidden_any.1, bf16[32,128]{1,0:T(8,128)(2,1)} %bitcast.3, bf16[64,512]{1,0:T(8,128)(2,1)} %wq_ref.1, ...), custom_call_target="tpu_custom_call" | custom-call | tf_op jit(solution)/shard_map/project_attend/pallas_call | solution.py:665
  118.7 1.8 %copy.14 = bf16[384,512]{1,0:T(8,128)(2,1)} copy(bf16[384,512]{1,0:T(8,128)(2,1)} %get-tuple-element.4) | data formatting | bytes 786432
  120.5 1.8 %copy.15 = bf16[384,512]{1,0:T(8,128)(2,1)} copy(bf16[384,512]{1,0:T(8,128)(2,1)} %get-tuple-element.5) | data formatting | bytes 786432

commit v3 on v2

--- a/solution.py
+++ b/solution.py
@@ -17,7 +17,9 @@
 MASKED = -1e30
 LAG_NEAR = 2
 LAG_FAR = 4
-UNROLL = 4
+GROUP = 2
+UNROLL = 3
+STACK = 2
 
 
 def clamp(value, low, high):
@@ -58,6 +60,8 @@
     psum,
     scores,
     tops,
+    totals,
+    stacked,
     hidden_sem,
     recv_a,
     send_a,
@@ -135,7 +139,7 @@
         kvb[0, 1, j * page_rows : (j + 1) * page_rows, :] = page_block[:, HEAD_WIDTH:]
     pl.semaphore_wait(barrier, len(greeted) + nh - 1)
 
-    low = nz * 5 // 16
+    low = nz // 4
     high = nz - 1 - low
 
     def reach(offset):
@@ -177,27 +181,30 @@
             x_up,
         ).wait_recv()
 
-    def kv_step(j):
+    def kv_half(j, half):
         reach_up = reach(j)
         back = nz + 1 - j
         reach_back = reach(back)
-        for half in range(2):
-
-            @pl.when(j <= reach_up)
+
+        @pl.when(j <= reach_up)
+        def _():
+            kv_wait(j, half)
+
+            @pl.when(j + 1 <= reach_up)
             def _():
-                kv_wait(j, half)
-
-                @pl.when(j + 1 <= reach_up)
-                def _():
-                    kv_forward(j, half).start()
-
-            @pl.when(back > reach_back)
+                kv_forward(j, half).start()
+
+        @pl.when(back > reach_back)
+        def _():
+            kv_wait(back, half)
+
+            @pl.when(back - 1 > reach_back)
             def _():
-                kv_wait(back, half)
-
-                @pl.when(back - 1 > reach_back)
-                def _():
-                    kv_backward(back, half).start()
+                kv_backward(back, half).start()
+
+    def kv_step(j):
+        kv_half(j, 0)
+        kv_half(j, 1)
 
     def position(i):
         distance = (i + 1) // 2
@@ -450,10 +457,11 @@
         def _():
             kv_step(m // 3)
 
-        late = m - 3 * kv_early
-        @pl.when((late > 0) & (late % 2 == 1) & (kv_early + (late + 1) // 2 <= nz))
-        def _():
-            kv_step(kv_early + (late + 1) // 2)
+        late = m - 3 * kv_early - 1
+
+        @pl.when((late >= 0) & (kv_early + late // 2 + 1 <= nz))
+        def _():
+            kv_half(kv_early + late // 2 + 1, late % 2)
 
         @pl.when(m >= LAG_FAR)
         def _():
@@ -466,12 +474,8 @@
 
         return carry
 
-    count = max(nz + LAG_FAR, last_z + 5)
-    assert count == nz + LAG_FAR or nz < 16
     lax.fori_loop(0, nz + LAG_FAR, weights_step, 0)
-    if last_z + 4 >= nz + LAG_FAR:
-        use_slots()
-    kv_next = kv_early + (nz + LAG_FAR - 1 - 3 * kv_early + 1) // 2 + 1
+    kv_next = kv_early + (nz + LAG_FAR - 1 - 3 * kv_early) // 2 + 1
 
     def service(limit):
         nonlocal kv_next
@@ -505,7 +509,9 @@
     for h in range(heads):
         u = acc[:, h * HEAD_WIDTH : (h + 1) * HEAD_WIDTH]
         turned = u * cosine[...] + pltpu.roll(u, HEAD_WIDTH // 2, 1) * sine[...]
-        query_ref[:, h * HEAD_WIDTH : (h + 1) * HEAD_WIDTH] = turned.astype(jnp.bfloat16)
+        turned = turned.astype(jnp.bfloat16)
+        query_ref[:, h * HEAD_WIDTH : (h + 1) * HEAD_WIDTH] = turned
+        stacked[h // STACK, (h % STACK) * tokens : (h % STACK + 1) * tokens, :] = turned
 
     service(first_late + 1)
 
@@ -513,86 +519,126 @@
     begin = start_col[...] - lane
     row = lax.broadcasted_iota(jnp.int32, (tokens, HEAD_WIDTH), 0)
     pieces = tokens // HEAD_WIDTH
-    ones = jnp.ones((tokens, HEAD_WIDTH), jnp.bfloat16)
-
-    def lanes_of(h):
-        return pl.ds(pl.multiple_of(h * HEAD_WIDTH, HEAD_WIDTH), HEAD_WIDTH)
-
-    def score(h, buffer, offset, top, causal):
+    done = min(first_late + 1, nz)
+
+    def at_hand(offset):
+        return offset <= low or offset > nz - low or max(offset, nz + 1 - offset) <= done
+
+    def groups(offsets):
+        found = []
+        for offset in offsets:
+            if found and len(found[-1]) < GROUP and found[-1][-1] + 1 == offset:
+                found[-1].append(offset)
+            else:
+                found.append([offset])
+        return found
+
+    early = groups([o for o in range(1, nz + 1) if at_hand(o)])
+    late = groups([o for o in range(1, nz + 1) if not at_hand(o)])
+
+    def rows_of(k):
+        return slice(k * tokens, (k + 1) * tokens)
+
+    def each(parts, body):
+        pairs = [part[0] for part in parts if len(part) == GROUP]
+
+        def one(k, carry):
+            offset = jnp.int32(pairs[0])
+            for other, start in enumerate(pairs):
+                offset = jnp.where(k == other, start, offset)
+            body(offset, GROUP)
+            return carry
+
+        if pairs:
+            lax.fori_loop(0, len(pairs), one, 0, unroll=UNROLL)
+        for part in parts:
+            if len(part) < GROUP:
+                body(part[0], len(part))
+
+    def block_of(offset, count, half):
+        return kvb[pl.ds(offset, count), half].reshape(count * tokens, HEAD_WIDTH)
+
+    def score(b, offset, count, own=False):
         block = lax.dot_general(
-            query_ref[:, lanes_of(h)],
-            kvb[offset, 0],
+            stacked[b],
+            block_of(offset, count, 0),
             (((1,), (1,)), ((), ())),
             preferred_element_type=jnp.float32,
         )
-        base = (me - offset) * tokens
-        for c in range(pieces):
-            visible = begin <= base + c * HEAD_WIDTH
-            if causal:
-                visible = visible & (lane + c * HEAD_WIDTH <= row)
-            part = block[:, c * HEAD_WIDTH : (c + 1) * HEAD_WIDTH]
-            part = jnp.where(visible, part, MASKED)
-            scores[buffer, offset, :, c * HEAD_WIDTH : (c + 1) * HEAD_WIDTH] = part
-            top = part if top is None else jnp.maximum(top, part)
-        return top
-
-    def score_early(h, buffer):
-        top = score(h, buffer, 0, None, True)
-
-        def one(k, top):
-            offset = jnp.where(k < low, k + 1, nz - 2 * low + 1 + k)
-            return score(h, buffer, offset, top, False)
-
-        tops[buffer] = lax.fori_loop(0, 2 * low, one, top, unroll=UNROLL)
-
-    def score_late(h, buffer):
-        return lax.fori_loop(
-            low + 1,
-            nz - low + 1,
-            lambda o, t: score(h, buffer, o, t, False),
-            tops[buffer],
-            unroll=UNROLL,
-        )
-
-    def finish_head(h, buffer, top):
-        top = jnp.broadcast_to(jnp.max(top, axis=1, keepdims=True), (tokens, HEAD_WIDTH))
-
-        def mix(offset, total):
-            weight = []
+        for g in range(count):
+            base = (me - offset - g) * tokens
+            seen = []
             for c in range(pieces):
-                part = scores[buffer, offset, :, c * HEAD_WIDTH : (c + 1) * HEAD_WIDTH]
-                weight.append(jnp.exp2((part - top) * factor).astype(jnp.bfloat16))
-            weight = jnp.concatenate(weight, axis=1)
-            value = jnp.concatenate([kvb[offset, 1], ones], axis=1)
-            return total + jnp.dot(weight, value, preferred_element_type=jnp.float32)
-
-        total = lax.fori_loop(
-            0,
-            nz + 1,
-            mix,
-            jnp.zeros((tokens, 2 * HEAD_WIDTH), jnp.float32),
-            unroll=UNROLL,
-        )
-        out_ref[:, lanes_of(h)] = (total[:, :HEAD_WIDTH] / total[:, HEAD_WIDTH:]).astype(
-            jnp.bfloat16
-        )
-
-    score_early(0, 0)
-    service(first_late + 2)
-    score_early(1, 1)
+                visible = begin <= base + c * HEAD_WIDTH
+                if own:
+                    visible = visible & (lane + c * HEAD_WIDTH <= row)
+                seen.append(visible)
+            for k in range(STACK):
+                top = None if own else tops[b, rows_of(k), :]
+                for c in range(pieces):
+                    first = (g * pieces + c) * HEAD_WIDTH
+                    part = block[rows_of(k), first : first + HEAD_WIDTH]
+                    part = jnp.where(seen[c], part, MASKED)
+                    scores[
+                        offset + g, rows_of(k), c * HEAD_WIDTH : (c + 1) * HEAD_WIDTH
+                    ] = part
+                    top = part if top is None else jnp.maximum(top, part)
+                tops[b, rows_of(k), :] = top
+
+    def level(b):
+        for k in range(STACK):
+            tops[b, rows_of(k), :] = jnp.broadcast_to(
+                jnp.max(tops[b, rows_of(k), :], axis=1, keepdims=True), (tokens, HEAD_WIDTH)
+            )
+
+    def mix(b, offset, count, own=False):
+        weight = []
+        for g in range(count):
+            for c in range(pieces):
+                part = scores[offset + g, :, c * HEAD_WIDTH : (c + 1) * HEAD_WIDTH]
+                weight.append(jnp.exp2((part - tops[b]) * factor).astype(jnp.bfloat16))
+        weight = jnp.concatenate(weight, axis=1)
+        value = block_of(offset, count, 1)
+        value = jnp.concatenate([value, jnp.ones_like(value)], axis=1)
+        product = jnp.dot(weight, value, preferred_element_type=jnp.float32)
+        totals[b] = product if own else totals[b] + product
+
+    def serve(j):
+        @pl.when(j <= nz)
+        def _():
+            kv_step(jnp.minimum(j, nz))
+
+    def attend_early(b, carry):
+        score(b, 0, 1, True)
+        each(early, lambda o, n: score(b, o, n))
+        level(b)
+        serve(done + 1 + 2 * b)
+        mix(b, 0, 1, True)
+        each(early, lambda o, n: mix(b, o, n))
+        serve(done + 2 + 2 * b)
+        return carry
+
+    def attend_late(b, carry):
+        if late:
+            before = tops[b]
+            each(late, lambda o, n: score(b, o, n))
+            level(b)
+            fade = jnp.exp2((before - tops[b]) * factor)
+            totals[b] = totals[b] * jnp.concatenate([fade, fade], axis=1)
+            each(late, lambda o, n: mix(b, o, n))
+        for k in range(STACK):
+            total = totals[b, rows_of(k), :]
+            h = b * STACK + k
+            out_ref[:, pl.ds(pl.multiple_of(h * HEAD_WIDTH, HEAD_WIDTH), HEAD_WIDTH)] = (
+                total[:, :HEAD_WIDTH] / total[:, HEAD_WIDTH:]
+            ).astype(jnp.bfloat16)
+        return carry
+
+    stacks = heads // STACK
+    lax.fori_loop(0, stacks, attend_early, 0)
+    kv_next = done + 1 + 2 * stacks
     service(nz)
-
-    def attend(h, carry):
-        buffer = h % 2
-
-        @pl.when(h >= 2)
-        def _():
-            score_early(h, buffer)
-
-        finish_head(h, buffer, score_late(h, buffer))
-        return carry
-
-    lax.fori_loop(0, heads, attend, 0)
+    lax.fori_loop(0, stacks, attend_late, 0)
 
     def finish(i, carry):
         @pl.when(goes_up(i))
@@ -654,6 +700,7 @@
     own_width = adapter_down_weight.shape[0]
     pages = logical_page_table.shape[1]
     requests = lengths.shape[0]
+    stacks = cols // HEAD_WIDTH // STACK
     kv = key_value_cache.reshape(pages, tokens // pages, 2 * HEAD_WIDTH)
     half = HEAD_WIDTH // 2
     freq = ROPE_BASE ** (-(np.arange(half, dtype=np.float64) * 2.0 / HEAD_WIDTH))
@@ -689,8 +736,10 @@
             pltpu.VMEM((tokens, HEAD_WIDTH), f32),
             pltpu.VMEM((tokens, HEAD_WIDTH), f32),
             pltpu.VMEM((nh, RANK, tokens), f32),
-            pltpu.VMEM((2, nz + 1, tokens, tokens), f32),
-            pltpu.VMEM((2, tokens, HEAD_WIDTH), f32),
+            pltpu.VMEM((nz + 1, STACK * tokens, tokens), f32),
+            pltpu.VMEM((stacks, STACK * tokens, HEAD_WIDTH), f32),
+            pltpu.VMEM((stacks, STACK * tokens, 2 * HEAD_WIDTH), f32),
+            pltpu.VMEM((stacks, STACK * tokens, HEAD_WIDTH), bf16),
             dma(()),
             dma((nz,)),
             dma((nz + 1,)),

time: 124 us -> 119 us (0.960)
  Pallas kernels: 116 us -> 112 us
    pallas_call x1, Pallas kernels: 116 us -> 112 us  [body(): pl.pallas_call(functools.partial(kernel, nz, nh), name='project_attend',...]
where the time goes in v3:
time: 119 us; the launch traced here: 117 us
  Pallas kernels  112 us (94%)
  local copies, waits for them, and re-layouts  5.26 us (4%)
    pallas_call x1, Pallas kernels, body(): pl.pallas_call(functools.partial(kernel, nz, nh), name='project_attend',...  112 us
    unnamed x2, local copies, waits for them, and re-layouts  3.53 us

profile of v3, /device:TPU:24, one launch (start us, length us, event | category | flops | bytes accessed | tf_op | source)
XLA Modules:
  0.0 117.4 jit_solution(16043816247012747768)
XLA Ops:
  0.6 1.7 %reshape.11.kv_ref = bf16[3,128,256]{2,1,0:T(8,128)(2,1)} reshape(bf16[384,2,128]{2,1,0:T(2,128)(2,1)} %param.15) | data formatting | bytes 393216 | tf_op jit(solution)/shard_map/reshape | solution.py:704
  2.4 111.5 %project_attend.1 = (bf16[384,512]{1,0:T(8,128)(2,1)}, bf16[384,512]{1,0:T(8,128)(2,1)}) custom-call(s32[16]{0:T(128)} %length_ref.1, s32[16]{0:T(128)} %prompt_adapter_ref.1, s32[1,3]{1,0:T(1,128)} %table_ref.1, bf16[384,4096]{1,0:T(8,128)(2,1)} %hidden_any.1, bf16[32,128]{1,0:T(8,128)(2,1)} %bitcast.3, bf16[64,512]{1,0:T(8,128)(2,1)} %wq_ref.1, ...), custom_call_target="tpu_custom_call" | custom-call | tf_op jit(solution)/shard_map/project_attend/pallas_call | solution.py:712
  113.9 1.8 %copy.14 = bf16[384,512]{1,0:T(8,128)(2,1)} copy(bf16[384,512]{1,0:T(8,128)(2,1)} %get-tuple-element.4) | data formatting | bytes 786432
  115.6 1.8 %copy.15 = bf16[384,512]{1,0:T(8,128)(2,1)} copy(bf16[384,512]{1,0:T(8,128)(2,1)} %get-tuple-element.5) | data formatting | bytes 786432

commit v4 on v3

--- a/solution.py
+++ b/solution.py
@@ -18,7 +18,7 @@
 LAG_NEAR = 2
 LAG_FAR = 4
 GROUP = 2
-UNROLL = 3
+UNROLL = 4
 STACK = 2
 
 
@@ -139,7 +139,7 @@
         kvb[0, 1, j * page_rows : (j + 1) * page_rows, :] = page_block[:, HEAD_WIDTH:]
     pl.semaphore_wait(barrier, len(greeted) + nh - 1)
 
-    low = nz // 4
+    low = nz * 5 // 16
     high = nz - 1 - low
 
     def reach(offset):
@@ -418,7 +418,7 @@
             body()
 
     last_z = 3 * (nz // 4) - 1 if nz % 4 == 0 else nz // 2
-    kv_early = nz // 5
+    gap = 4 if nz >= 16 else 1
 
     def weights_step(m, carry):
         distance = 2 * (m // 3) + m % 3
@@ -450,18 +450,12 @@
 
         at(m, LAG_FAR + 1, rotation)
         at(m, last_z, make_share)
-        at(m, last_z + 2, sum_share)
-        at(m, last_z + 4, use_slots)
-
-        @pl.when((m % 3 == 0) & (m >= 3) & (m // 3 <= kv_early))
-        def _():
-            kv_step(m // 3)
-
-        late = m - 3 * kv_early - 1
-
-        @pl.when((late >= 0) & (kv_early + late // 2 + 1 <= nz))
-        def _():
-            kv_half(kv_early + late // 2 + 1, late % 2)
+        at(m, last_z + gap, sum_share)
+        at(m, last_z + 2 * gap, use_slots)
+
+        @pl.when((m >= 1) & ((m + 1) // 2 <= nz))
+        def _():
+            kv_half((m + 1) // 2, (m + 1) % 2)
 
         @pl.when(m >= LAG_FAR)
         def _():
@@ -475,7 +469,10 @@
         return carry
 
     lax.fori_loop(0, nz + LAG_FAR, weights_step, 0)
-    kv_next = kv_early + (nz + LAG_FAR - 1 - 3 * kv_early) // 2 + 1
+    halves = nz + LAG_FAR - 1
+    kv_next = (halves + 1) // 2 + 1
+    if halves % 2 == 1 and (halves + 1) // 2 <= nz:
+        kv_half(jnp.int32((halves + 1) // 2), 1)
 
     def service(limit):
         nonlocal kv_next
@@ -680,6 +677,17 @@
     lax.fori_loop(0, nz + 1, kv_finish, 0)
     for half in range(2):
         kv_cross(half).wait_send()
+
+
+def relay(first_ref, second_ref, first_out, second_out, sem):
+    copies = [
+        pltpu.make_async_copy(first_ref, first_out, sem.at[0]),
+        pltpu.make_async_copy(second_ref, second_out, sem.at[1]),
+    ]
+    for copy in copies:
+        copy.start()
+    for copy in copies:
+        copy.wait()
 
 
 def body(
@@ -709,7 +717,7 @@
     vmem = pl.BlockSpec(memory_space=pltpu.VMEM)
     dma = pltpu.SemaphoreType.DMA
     bf16, f32, i32 = jnp.bfloat16, jnp.float32, jnp.int32
-    return pl.pallas_call(
+    results = pl.pallas_call(
         functools.partial(kernel, nz, nh),
         name="project_attend",
         out_shape=(
@@ -771,6 +779,18 @@
         kv,
         freq,
     )
+    anywhere = pl.BlockSpec(memory_space=pl.ANY)
+    return pl.pallas_call(
+        relay,
+        name="relay",
+        out_shape=(
+            jax.ShapeDtypeStruct((tokens, cols), bf16),
+            jax.ShapeDtypeStruct((tokens, cols), bf16),
+        ),
+        in_specs=[anywhere] * 2,
+        out_specs=(anywhere, anywhere),
+        scratch_shapes=[dma((2,))],
+    )(*results)
 
 
 def solution(mesh):

time: 119 us -> 138 us (1.16)
  the two profiles are of different devices: /device:TPU:24 before, /device:TPU:1 now
where the time goes in v4:
time: 138 us
  Pallas kernels  136 us (99%)
  local copies, waits for them, and re-layouts  1.73 us (1%)
    pallas_call x1, Pallas kernels, body(): pl.pallas_call(functools.partial(kernel, nz, nh), name='project_attend',...  111 us
    pallas_call x1, Pallas kernels, body(): pl.pallas_call(relay, name='relay', out_shape=(jax.ShapeDtypeStruct((toke...  24.9 us

profile of v4, /device:TPU:1, one launch (start us, length us, event | category | flops | bytes accessed | tf_op | source)
XLA Modules:
  0.0 138.2 jit_solution(16482393458496384808)
XLA Ops:
  0.6 1.7 %reshape.11.kv_ref = bf16[3,128,256]{2,1,0:T(8,128)(2,1)} reshape(bf16[384,2,128]{2,1,0:T(2,128)(2,1)} %param.15) | data formatting | bytes 393216 | tf_op jit(solution)/shard_map/reshape | solution.py:712
  2.4 110.9 %project_attend.1 = (bf16[384,512]{1,0:T(8,128)(2,1)}, bf16[384,512]{1,0:T(8,128)(2,1)}) custom-call(s32[16]{0:T(128)} %length_ref.1, s32[16]{0:T(128)} %prompt_adapter_ref.1, s32[1,3]{1,0:T(1,128)} %table_ref.1, bf16[384,4096]{1,0:T(8,128)(2,1)} %hidden_any.1, bf16[32,128]{1,0:T(8,128)(2,1)} %bitcast.3, bf16[64,512]{1,0:T(8,128)(2,1)} %wq_ref.1, ...), custom_call_target="tpu_custom_call" | custom-call | tf_op jit(solution)/shard_map/project_attend/pallas_call | solution.py:720
  113.3 24.9 %relay.1 = (bf16[384,512]{1,0:T(8,128)(2,1)}, bf16[384,512]{1,0:T(8,128)(2,1)}) custom-call(bf16[384,512]{1,0:T(8,128)(2,1)} %get-tuple-element.4.first_ref, bf16[384,512]{1,0:T(8,128)(2,1)} %get-tuple-element.5.second_ref), custom_call_target="tpu_custom_call" | custom-call | tf_op jit(solution)/shard_map/relay/pallas_call | solution.py:783

commit v5 on v4

--- a/solution.py
+++ b/solution.py
@@ -679,15 +679,9 @@
         kv_cross(half).wait_send()
 
 
-def relay(first_ref, second_ref, first_out, second_out, sem):
-    copies = [
-        pltpu.make_async_copy(first_ref, first_out, sem.at[0]),
-        pltpu.make_async_copy(second_ref, second_out, sem.at[1]),
-    ]
-    for copy in copies:
-        copy.start()
-    for copy in copies:
-        copy.wait()
+def relay(first_ref, second_ref, first_out, second_out):
+    first_out[...] = first_ref[...]
+    second_out[...] = second_ref[...]
 
 
 def body(
@@ -779,7 +773,6 @@
         kv,
         freq,
     )
-    anywhere = pl.BlockSpec(memory_space=pl.ANY)
     return pl.pallas_call(
         relay,
         name="relay",
@@ -787,9 +780,8 @@
             jax.ShapeDtypeStruct((tokens, cols), bf16),
             jax.ShapeDtypeStruct((tokens, cols), bf16),
         ),
-        in_specs=[anywhere] * 2,
-        out_specs=(anywhere, anywhere),
-        scratch_shapes=[dma((2,))],
+        in_specs=[vmem] * 2,
+        out_specs=(vmem, vmem),
     )(*results)
 
 

time: 138 us -> 115 us (0.83)
  Pallas kernels: 136 us -> 113 us
    pallas_call x1, Pallas kernels: 24.9 us -> 2.02 us  [body(): pl.pallas_call(relay, name='relay', out_shape=(jax.ShapeDtypeStruct((toke...]
where the time goes in v5:
time: 115 us
  Pallas kernels  113 us (98%)
  local copies, waits for them, and re-layouts  1.73 us (2%)
    pallas_call x1, Pallas kernels, body(): pl.pallas_call(functools.partial(kernel, nz, nh), name='project_attend',...  111 us

profile of v5, /device:TPU:1, one launch (start us, length us, event | category | flops | bytes accessed | tf_op | source)
XLA Modules:
  0.0 115.3 jit_solution(1112250804035318625)
XLA Ops:
  0.6 1.7 %reshape.11.kv_ref = bf16[3,128,256]{2,1,0:T(8,128)(2,1)} reshape(bf16[384,2,128]{2,1,0:T(2,128)(2,1)} %param.15) | data formatting | bytes 393216 | tf_op jit(solution)/shard_map/reshape | solution.py:706
  2.4 110.9 %project_attend.1 = (bf16[384,512]{1,0:T(8,128)(2,1)}, bf16[384,512]{1,0:T(8,128)(2,1)}) custom-call(s32[16]{0:T(128)} %length_ref.1, s32[16]{0:T(128)} %prompt_adapter_ref.1, s32[1,3]{1,0:T(1,128)} %table_ref.1, bf16[384,4096]{1,0:T(8,128)(2,1)} %hidden_any.1, bf16[32,128]{1,0:T(8,128)(2,1)} %bitcast.3, bf16[64,512]{1,0:T(8,128)(2,1)} %wq_ref.1, ...), custom_call_target="tpu_custom_call" | custom-call | tf_op jit(solution)/shard_map/project_attend/pallas_call | solution.py:714
  113.3 2.0 %relay.1 = (bf16[384,512]{1,0:T(8,128)(2,1)}, bf16[384,512]{1,0:T(8,128)(2,1)}) custom-call(bf16[384,512]{1,0:T(8,128)(2,1)} %get-tuple-element.4.first_ref, bf16[384,512]{1,0:T(8,128)(2,1)} %get-tuple-element.5.second_ref), custom_call_target="tpu_custom_call" | custom-call | tf_op jit(solution)/shard_map/relay/pallas_call | solution.py:776
